TPU v7x, 128 devices: a whole 4x4x4 slice. The times are simulated.
128 devices in a mesh: modes: 32 (over y, z, x_lo), mesh: 4 (over x_hi, core).
Axes of the slice: x: 4 (x_hi: 2, x_lo: 2; x = x_hi * 2 + x_lo), y: 4, z: 4, core: 2. Of those that a mesh axis runs over, the one named last changes fastest.
Arguments:
- velocity: float32 [3, 64, 2, 12288], P(None, 'modes', None, 'mesh'), may hold values from -0.4 to 0.4
- blocks: float32 [96, 9, 128, 128], P('mesh'), may hold values from -0.09375 to 0.09375
- neighbours: int32 [96, 9], P('mesh'), may hold values from 0 to 95, as said below
- element_derivative: float32 [2, 16, 16], replicated, may hold values from -1.5 to 1.5
Outputs:
- advanced: float32 [3, 64, 2, 12288], P(None, 'modes', None, 'mesh')
Inputs may be any that keep to these rules, and one draw needn't show every extreme that they name: neighbours[r, j] differs from r by at most 2; neighbours[r, 4] = r, and neighbours[r, 0] = r - 2, neighbours[r, 8] = r + 2 where these lie in range, else the nearest block row in range.
All inputs are finite; a program needn't handle non-finite values.
Results may differ from a plain program's by a relative error of at most 0.0003.
Values sent between devices are 32-bit elements; how exact they have to be, the bound alone decides.
No kernel may reach another device: no remote copies, remote signals or barrier semaphores. Data moves between devices by JAX's collectives and lax.ppermute only.
A program may use at most 192 MiB of HBM per device.

v0:
```python
import jax
import jax.numpy as jnp
from jax import lax
from jax.sharding import PartitionSpec as P

ELEM = 16
HW = 2
SWEEPS = 3
STEPS = 5


PRECISE = lax.Precision.HIGHEST
PRODUCT_PAIRS = ((0, 0), (0, 1), (0, 2), (1, 1), (1, 2), (2, 2))
VISCOSITY = 0.1
TIME_STEP = 0.2
HALF_WIDTH = 0.6
SPAN_WAVE = 1.0 / 16.0


def padded(cells, sides, width):
    for axis, dim in sides:
        count = lax.axis_size(axis)
        ends = count - 1
        head = lax.slice_in_dim(cells, 0, width, axis=dim)
        tail = lax.slice_in_dim(cells, cells.shape[dim] - width, cells.shape[dim], axis=dim)
        cells = jnp.concatenate(
            [
                lax.ppermute(tail, axis, [(i, (i + 1) % count) for i in range(ends)]),
                cells,
                lax.ppermute(head, axis, [((i + 1) % count, i) for i in range(ends)]),
            ],
            axis=dim,
        )
    return cells


def pair_slot(left_index, right_index):
    return PRODUCT_PAIRS.index((min(left_index, right_index), max(left_index, right_index)))


def tables(mode_count):
    points = 2 * mode_count
    z_index = jnp.arange(points, dtype=jnp.int32)[:, None]
    k_index = jnp.arange(mode_count, dtype=jnp.int32)[None, :]
    angles = 2.0 * jnp.pi / points * (z_index * k_index % points).astype(jnp.float32)
    cosine = jnp.cos(angles)
    sine = jnp.sin(angles)
    weights = jnp.where(k_index == 0, 1.0, 2.0).astype(jnp.float32)
    inverse = jnp.stack([weights * cosine, -weights * sine], axis=2)
    forward = jnp.stack([cosine.T, -sine.T], axis=1) / points
    wave = jnp.arange(mode_count, dtype=jnp.float32) * SPAN_WAVE
    return (inverse, forward, wave)


def plane_derivative(values, matrix):
    full_shape = values.shape
    grouped = values.reshape(full_shape[:-1] + (full_shape[-1] // ELEM, ELEM))
    return jnp.einsum("ij,...ej->...ei", matrix, grouped, precision=PRECISE).reshape(full_shape)


def assemble(spectra, wave, element_derivative):
    terms = []
    for axis_index in range(3):
        along = spectra[pair_slot(axis_index, 2)]
        spanwise = jnp.stack([-wave[:, None] * along[:, 1], wave[:, None] * along[:, 0]], axis=1)
        planar = plane_derivative(spectra[pair_slot(axis_index, 0)], element_derivative[0])
        planar = planar + plane_derivative(spectra[pair_slot(axis_index, 1)], element_derivative[1])
        terms.append(spanwise + planar)
    return jnp.stack(terms)


def chebyshev(right_side, diagonal_shift, apply_coupling):
    sigma_ratio = diagonal_shift / HALF_WIDTH
    ratio_old = 1.0 / sigma_ratio
    solution = jnp.zeros_like(right_side)
    residual = right_side
    direction = right_side / diagonal_shift
    for sweep_index in range(SWEEPS):
        solution = solution + direction
        residual = residual - (diagonal_shift * direction + apply_coupling(direction))
        ratio_new = 1.0 / (2.0 * sigma_ratio - ratio_old)
        direction = ratio_new * ratio_old * direction + 2.0 * ratio_new / HALF_WIDTH * residual
        ratio_old = ratio_new
    return solution + direction


def on_device(velocity, blocks, neighbours, element_derivative):
    modes_local = velocity.shape[1]
    modes_total = modes_local * lax.axis_size("modes")
    inverse, forward, wave_total = tables(modes_total)
    wave = lax.dynamic_slice_in_dim(wave_total, lax.axis_index("modes") * modes_local, modes_local)
    diagonal_shift = (1.0 + VISCOSITY * wave * wave)[None, :, None, None]
    block_rows = blocks.shape[0]
    block_size = blocks.shape[2]
    local_rows = neighbours - lax.axis_index("mesh") * block_rows + HW

    def apply_coupling(vector_field):
        full_shape = vector_field.shape
        rows = vector_field.reshape(-1, block_rows, block_size)
        extended = padded(rows, (("mesh", 1),), HW)
        picked = extended[:, local_rows, :]
        coupled = jnp.einsum("cnjq,njpq->cnp", picked, blocks, precision=PRECISE)
        return coupled.reshape(full_shape)

    state = velocity
    for time_index in range(STEPS):
        columns = lax.all_to_all(state, "modes", split_axis=3, concat_axis=1, tiled=True)
        physical = jnp.einsum("zkr,ckrp->czp", inverse, columns, precision=PRECISE)
        products = jnp.stack([physical[a] * physical[b] for a, b in PRODUCT_PAIRS])
        spectra = jnp.einsum("krz,mzp->mkrp", forward, products, precision=PRECISE)
        returned = lax.all_to_all(spectra, "modes", split_axis=1, concat_axis=3, tiled=True)
        forcing = assemble(returned, wave, element_derivative)
        right_side = state - TIME_STEP * forcing
        state = chebyshev(right_side, diagonal_shift, apply_coupling)
    return state


def solution(mesh):
    in_specs = (P(None, "modes", None, "mesh"), P("mesh", None, None, None), P("mesh", None), P())
    out_specs = P(None, "modes", None, "mesh")
    return jax.shard_map(
        on_device, mesh=mesh, in_specs=in_specs, out_specs=out_specs, check_vma=False
    )
```

profile of v0, /device:TPU:1, one launch (start us, length us, event | category | flops | bytes accessed | tf_op | source)
XLA Modules:
  0.0 744.5 jit_solution(9310667632953397005)
XLA Ops:
  35.4 11.2 %reshape.1446 = f32[3072,2,2,3]{3,2,1,0:T(2,128)} reshape(f32[32,1152]{1,0:T(8,128)S(1)} %reduce) | data formatting | bytes 294912
  93.3 15.3 %convolution_bitcast_fusion.19 = f32[12,24,128]{2,0,1:T(8,128)S(1)} fusion(f32[12,24,9,128]{3,0,2,1:T(8,128)S(1)} %bitcast.560, f32[24,9,128,128]{3,2,1,0:T(8,128)} %param.5), kind=kOutput, calls=%fused_computation.34 | convolution fusion | flops 509607936 | bytes 15630336 | tf_op jit(solution)/shard_map/cnjq,njpq->cnp/dot_general | solution.py:102
  118.6 15.3 %convolution_bitcast_fusion.18 = f32[12,24,128]{2,0,1:T(8,128)S(1)} fusion(f32[12,24,9,128]{3,0,2,1:T(8,128)S(1)} %bitcast.561, f32[24,9,128,128]{3,2,1,0:T(8,128)} %param.5), kind=kOutput, calls=%fused_computation.33 | convolution fusion | flops 509607936 | bytes 15630336 | tf_op jit(solution)/shard_map/cnjq,njpq->cnp/dot_general | solution.py:102
  143.9 15.3 %convolution_bitcast_fusion.17 = f32[12,24,128]{2,0,1:T(8,128)S(1)} fusion(f32[12,24,9,128]{3,0,2,1:T(8,128)S(1)} %bitcast.562, f32[24,9,128,128]{3,2,1,0:T(8,128)} %param.5), kind=kOutput, calls=%fused_computation.32 | convolution fusion | flops 509607936 | bytes 15630336 | tf_op jit(solution)/shard_map/cnjq,njpq->cnp/dot_general | solution.py:102
  186.1 11.2 %reshape.1448 = f32[3072,2,2,3]{3,2,1,0:T(2,128)} reshape(f32[32,1152]{1,0:T(8,128)S(1)} %reduce.1) | data formatting | bytes 294912
  206.9 13.6 %all_to_all.166 = f32[6,64,2,96]{3,2,0,1:T(2,128)S(1)} all-to-all(f32[6,64,2,96]{3,2,0,1:T(2,128)S(1)} %copy.381), channel_id=1, replica_groups=mesh['modes'=32,'mesh'=4] {'modes'}, dimensions={1} | all-to-all | bytes 589824 | tf_op jit(solution)/shard_map/all_to_all | solution.py:111
  239.2 15.3 %convolution_bitcast_fusion.16 = f32[12,24,128]{2,0,1:T(8,128)S(1)} fusion(f32[12,24,9,128]{3,0,2,1:T(8,128)S(1)} %bitcast.563, f32[24,9,128,128]{3,2,1,0:T(8,128)} %param.5), kind=kOutput, calls=%fused_computation.31 | convolution fusion | flops 509607936 | bytes 15630336 | tf_op jit(solution)/shard_map/cnjq,njpq->cnp/dot_general | solution.py:102
  264.5 15.3 %convolution_bitcast_fusion.15 = f32[12,24,128]{2,0,1:T(8,128)S(1)} fusion(f32[12,24,9,128]{3,0,2,1:T(8,128)S(1)} %bitcast.564, f32[24,9,128,128]{3,2,1,0:T(8,128)} %param.5), kind=kOutput, calls=%fused_computation.30 | convolution fusion | flops 509607936 | bytes 15630336 | tf_op jit(solution)/shard_map/cnjq,njpq->cnp/dot_general | solution.py:102
  289.8 15.3 %convolution_bitcast_fusion.14 = f32[12,24,128]{2,0,1:T(8,128)S(1)} fusion(f32[12,24,9,128]{3,0,2,1:T(8,128)S(1)} %bitcast.565, f32[24,9,128,128]{3,2,1,0:T(8,128)} %param.5), kind=kOutput, calls=%fused_computation.29 | convolution fusion | flops 509607936 | bytes 15630336 | tf_op jit(solution)/shard_map/cnjq,njpq->cnp/dot_general | solution.py:102
  332.0 11.2 %reshape.1450 = f32[3072,2,2,3]{3,2,1,0:T(2,128)} reshape(f32[32,1152]{1,0:T(8,128)S(1)} %reduce.2) | data formatting | bytes 294912
  352.8 13.6 %all_to_all.168 = f32[6,64,2,96]{3,2,0,1:T(2,128)S(1)} all-to-all(f32[6,64,2,96]{3,2,0,1:T(2,128)S(1)} %copy.406), channel_id=1, replica_groups=mesh['modes'=32,'mesh'=4] {'modes'}, dimensions={1} | all-to-all | bytes 589824 | tf_op jit(solution)/shard_map/all_to_all | solution.py:111
  385.1 15.3 %convolution_bitcast_fusion.13 = f32[12,24,128]{2,0,1:T(8,128)S(1)} fusion(f32[12,24,9,128]{3,0,2,1:T(8,128)S(1)} %bitcast.566, f32[24,9,128,128]{3,2,1,0:T(8,128)} %param.5), kind=kOutput, calls=%fused_computation.28 | convolution fusion | flops 509607936 | bytes 15630336 | tf_op jit(solution)/shard_map/cnjq,njpq->cnp/dot_general | solution.py:102
  410.4 15.3 %convolution_bitcast_fusion.12 = f32[12,24,128]{2,0,1:T(8,128)S(1)} fusion(f32[12,24,9,128]{3,0,2,1:T(8,128)S(1)} %bitcast.567, f32[24,9,128,128]{3,2,1,0:T(8,128)} %param.5), kind=kOutput, calls=%fused_computation.27 | convolution fusion | flops 509607936 | bytes 15630336 | tf_op jit(solution)/shard_map/cnjq,njpq->cnp/dot_general | solution.py:102
  435.7 15.3 %convolution_bitcast_fusion.11 = f32[12,24,128]{2,0,1:T(8,128)S(1)} fusion(f32[12,24,9,128]{3,0,2,1:T(8,128)S(1)} %bitcast.568, f32[24,9,128,128]{3,2,1,0:T(8,128)} %param.5), kind=kOutput, calls=%fused_computation.26 | convolution fusion | flops 509607936 | bytes 15630336 | tf_op jit(solution)/shard_map/cnjq,njpq->cnp/dot_general | solution.py:102
  477.9 11.2 %reshape.1452 = f32[3072,2,2,3]{3,2,1,0:T(2,128)} reshape(f32[32,1152]{1,0:T(8,128)S(1)} %reduce.3) | data formatting | bytes 294912
  498.7 13.6 %all_to_all.170 = f32[6,64,2,96]{3,2,0,1:T(2,128)S(1)} all-to-all(f32[6,64,2,96]{3,2,0,1:T(2,128)S(1)} %copy.431), channel_id=1, replica_groups=mesh['modes'=32,'mesh'=4] {'modes'}, dimensions={1} | all-to-all | bytes 589824 | tf_op jit(solution)/shard_map/all_to_all | solution.py:111
  531.0 15.3 %convolution_bitcast_fusion.10 = f32[12,24,128]{2,0,1:T(8,128)S(1)} fusion(f32[12,24,9,128]{3,0,2,1:T(8,128)S(1)} %bitcast.569, f32[24,9,128,128]{3,2,1,0:T(8,128)} %param.5), kind=kOutput, calls=%fused_computation.25 | convolution fusion | flops 509607936 | bytes 15630336 | tf_op jit(solution)/shard_map/cnjq,njpq->cnp/dot_general | solution.py:102
  556.3 15.3 %convolution_bitcast_fusion.9 = f32[12,24,128]{2,0,1:T(8,128)S(1)} fusion(f32[12,24,9,128]{3,0,2,1:T(8,128)S(1)} %bitcast.570, f32[24,9,128,128]{3,2,1,0:T(8,128)} %param.5), kind=kOutput, calls=%fused_computation.24 | convolution fusion | flops 509607936 | bytes 15630336 | tf_op jit(solution)/shard_map/cnjq,njpq->cnp/dot_general | solution.py:102
  581.6 15.3 %convolution_bitcast_fusion.8 = f32[12,24,128]{2,0,1:T(8,128)S(1)} fusion(f32[12,24,9,128]{3,0,2,1:T(8,128)S(1)} %bitcast.571, f32[24,9,128,128]{3,2,1,0:T(8,128)} %param.5), kind=kOutput, calls=%fused_computation.23 | convolution fusion | flops 509607936 | bytes 15630336 | tf_op jit(solution)/shard_map/cnjq,njpq->cnp/dot_general | solution.py:102
  623.9 11.2 %reshape.1454 = f32[3072,2,2,3]{3,2,1,0:T(2,128)} reshape(f32[32,1152]{1,0:T(8,128)S(1)} %reduce.4) | data formatting | bytes 294912
  644.6 13.6 %all_to_all.172 = f32[6,64,2,96]{3,2,0,1:T(2,128)S(1)} all-to-all(f32[6,64,2,96]{3,2,0,1:T(2,128)S(1)} %copy.456), channel_id=1, replica_groups=mesh['modes'=32,'mesh'=4] {'modes'}, dimensions={1} | all-to-all | bytes 589824 | tf_op jit(solution)/shard_map/all_to_all | solution.py:111
  676.9 15.3 %convolution_bitcast_fusion.7 = f32[12,24,128]{2,0,1:T(8,128)S(1)} fusion(f32[12,24,9,128]{3,0,2,1:T(8,128)S(1)} %bitcast.572, f32[24,9,128,128]{3,2,1,0:T(8,128)} %param.5), kind=kOutput, calls=%fused_computation.22 | convolution fusion | flops 509607936 | bytes 15630336 | tf_op jit(solution)/shard_map/cnjq,njpq->cnp/dot_general | solution.py:102
  702.3 15.3 %convolution_bitcast_fusion.6 = f32[12,24,128]{2,0,1:T(8,128)S(1)} fusion(f32[12,24,9,128]{3,0,2,1:T(8,128)S(1)} %bitcast.573, f32[24,9,128,128]{3,2,1,0:T(8,128)} %param.5), kind=kOutput, calls=%fused_computation.21 | convolution fusion | flops 509607936 | bytes 15630336 | tf_op jit(solution)/shard_map/cnjq,njpq->cnp/dot_general | solution.py:102
  727.5 15.3 %convolution_bitcast_fusion.5 = f32[12,24,128]{2,0,1:T(8,128)S(1)} fusion(f32[12,24,9,128]{3,0,2,1:T(8,128)S(1)} %bitcast.559, f32[24,9,128,128]{3,2,1,0:T(8,128)} %param.5), kind=kOutput, calls=%fused_computation.20 | convolution fusion | flops 509607936 | bytes 15630336 | tf_op jit(solution)/shard_map/cnjq,njpq->cnp/dot_general | solution.py:102
  (407 shorter events, 401.8 us)
Async XLA Ops:
  16.4 17.5 %all-to-all-start = ((f32[32,1,1152]{2,1,0:T(1,128)}), f32[32,1,1152]{2,1,0:T(1,128)S(1)}, u32[]{:S(2)}, u32[]{:S(2)}) async-start(f32[32,1,1152]{2,1,0:T(1,128)} %reshape.1445), calls=%async_computation | async-start | bytes 294912 | tf_op jit(solution)/shard_map/all_to_all | solution.py:107
  57.0 13.6 %all-to-all-start.1 = ((f32[6,64,2,96]{3,2,0,1:T(2,128)}), f32[6,64,2,96]{3,2,0,1:T(2,128)S(1)}, u32[]{:S(2)}, u32[]{:S(2)}) async-start(f32[6,64,2,96]{3,2,0,1:T(2,128)} %copy.355), calls=%async_computation.1 | async-start | bytes 786432 | tf_op jit(solution)/shard_map/all_to_all | solution.py:111
  78.3 9.4 %collective-permute-start = (f32[12,2,128]{2,0,1:T(8,128)S(1)}, f32[12,2,128]{2,0,1:T(8,128)S(1)}, u32[]{:S(2)}, u32[]{:S(2)}) collective-permute-start(f32[12,2,128]{2,0,1:T(8,128)S(1)} %get-tuple-element.79), channel_id=1, source_target_pairs={{0,1},{1,2},{2,3},{4,5},{5,6},{6,7},{8,9},{9,10},{10,11},{12,13},{... | collective-permute-start | bytes 36872 | tf_op jit(solution)/shard_map/ppermute | solution.py:28
  85.7 6.6 collective-permute-start.1
  111.1 6.6 collective-permute-start.3
  136.3 6.6 collective-permute-start.5
  228.1 5.8 collective-permute-start.6
  231.6 6.6 collective-permute-start.7
  257.0 6.6 collective-permute-start.9
  280.3 4.5 collective-permute-start.10
  282.3 6.6 collective-permute-start.11
  374.1 5.8 collective-permute-start.12
  377.6 6.6 collective-permute-start.13
  402.9 6.6 collective-permute-start.15
  428.2 6.6 collective-permute-start.17
  520.0 5.8 collective-permute-start.18
  523.5 6.6 collective-permute-start.19
  548.8 6.6 collective-permute-start.21
  574.1 6.6 collective-permute-start.23
  665.9 5.7 collective-permute-start.24
  669.4 6.6 collective-permute-start.25
  694.7 6.6 collective-permute-start.27
  718.1 4.6 collective-permute-start.28
  720.0 6.6 collective-permute-start.29
  (11 other events, 70.7 us)
where the time goes:
time: 755 us; the launch traced here: 745 us
  matrix products  257 us (34%)
  local copies, waits for them, and re-layouts  204 us (27%)
  blocking collectives  97.9 us (13%)
  starting transfers between devices  91 us (12%)
  waiting for transfers between devices  78.3 us (10%)
  other arithmetic  13.1 us (2%)
    dot_general x15, matrix products, apply_coupling(): coupled = jnp.einsum('cnjq,njpq->cnp', picked, blocks, precision=PRECISE)  229 us
    unnamed x17, local copies, waits for them, and re-layouts  106 us
    ppermute x15, waiting for transfers between devices, padded(): lax.ppermute(head, axis, [((i + 1) % count, i) for i in range(ends)])  62.2 us
    all_to_all x4, blocking collectives, on_device(): lax.all_to_all(spectra, 'modes', split_axis=1, concat_axis=3, tiled=True)  54.4 us
    all_to_all x4, blocking collectives, on_device(): lax.all_to_all(state, 'modes', split_axis=3, concat_axis=1, tiled=True)  43.5 us
    ppermute x15, starting transfers between devices, padded(): lax.ppermute(tail, axis, [(i, (i + 1) % count) for i in range(ends)])  40.7 us
    all_to_all x6, local copies, waits for them, and re-layouts, on_device(): lax.all_to_all(state, 'modes', split_axis=3, concat_axis=1, tiled=True)  39.4 us
    ppermute x15, starting transfers between devices, padded(): lax.ppermute(head, axis, [((i + 1) % count, i) for i in range(ends)])  35.9 us
  transfers between devices with their start and end apart: 32, of which 17 were waited for; matrix products, arithmetic and copies ran while one was open for 0% of the time, Pallas kernels for 0%

commit v1 on v0

v1 whole, which is shorter than its diff:
```python
import jax
import jax.numpy as jnp
import numpy as np
from jax import lax
from jax.experimental import pallas as pl
from jax.experimental.pallas import tpu as pltpu
from jax.sharding import Mesh
from jax.sharding import PartitionSpec as P

ELEM = 16
HW = 2
SWEEPS = 3
STEPS = 5
BLK = 128
BAND = 2 * HW + 1

VISCOSITY = 0.1
TIME_STEP = 0.2
HALF_WIDTH = 0.6
SPAN_WAVE = 1.0 / 16.0

MODES = 64
POINTS = 2 * MODES
PAIRS = ((0, 0), (0, 1), (0, 2), (1, 1), (1, 2), (2, 2))
AXES = ("y", "z", "xl", "xh", "co")
TEAM = 8
OWN = 6
VEC = 48
EDGE = 2 * HW
WIN = 3 * OWN
ROWS = OWN + 2 * EDGE
LOCAL = 24

F32 = jnp.float32
BF16 = jnp.bfloat16


def device_of(y, z, xl, xh, co):
    return (((y * 4 + z) * 2 + xl) * 2 + xh) * 2 + co


def team_devices(rank):
    s, q = divmod(rank, 4)
    xh, co = divmod(s, 2)
    y = q if co == 0 else 3 - q
    return [device_of(y, z, xl, xh, co) for z in range(4) for xl in range(2)]


def shift_pairs(step):
    return [
        (a, b)
        for rank in range(16)
        if 0 <= rank + step < 16
        for a, b in zip(team_devices(rank), team_devices(rank + step))
    ]


def seam_pairs():
    pairs = []
    for rank in (3, 7, 11):
        for a, b in zip(team_devices(rank), team_devices(rank + 1)):
            pairs += [(a, b), (b, a)]
    return pairs


def split_np(x):
    hi = x.astype(BF16)
    lo = (x - hi.astype(np.float64)).astype(BF16)
    return hi, lo


def mode_rows():
    modes, parts = [], []
    for member in range(TEAM):
        for y in range(4):
            for m in range(2):
                for r in range(2):
                    modes.append(2 * (y * 8 + member) + m)
                    parts.append(r)
    return np.array(modes), np.array(parts)


def tables():
    modes, parts = mode_rows()
    z = np.arange(POINTS)
    angle = 2.0 * np.pi / POINTS * ((z[:, None] * modes[None, :]) % POINTS)
    cosine, sine = np.cos(angle), np.sin(angle)
    weight = np.where(modes == 0, 1.0, 2.0)
    inverse = np.where(parts == 0, cosine, -sine) * weight
    forward = (np.where(parts == 0, cosine, -sine) / POINTS).T
    wave = modes * SPAN_WAVE
    other = (np.where(parts == 0, -sine, cosine) / POINTS).T
    spanwise = np.where(parts == 0, -wave, wave)[:, None] * other
    both = -TIME_STEP * np.concatenate([forward, spanwise], axis=1)
    ihi, ilo = split_np(inverse)
    fhi, flo = split_np(both)
    return (
        np.concatenate([ihi, ihi, ilo], axis=1),
        np.concatenate([fhi, flo], axis=0),
    )


def solve_coefficients():
    shift = 1.0 + VISCOSITY * (np.arange(MODES) * SPAN_WAVE) ** 2
    sigma = shift / HALF_WIDTH
    old = 1.0 / sigma
    width = SWEEPS + 1
    residual = np.zeros((MODES, width))
    residual[:, 0] = 1.0
    direction = residual / shift[:, None]
    total = np.zeros((MODES, width))
    for _ in range(SWEEPS):
        total = total + direction
        moved = np.concatenate([np.zeros((MODES, 1)), direction[:, :-1]], axis=1)
        residual = residual - (shift[:, None] * direction + moved)
        new = 1.0 / (2.0 * sigma - old)
        direction = (new * old)[:, None] * direction + (2.0 * new / HALF_WIDTH)[:, None] * residual
        old = new
    total = total + direction
    modes, _ = mode_rows()
    out = np.zeros((TEAM, VEC, BLK), np.float32)
    for member in range(TEAM):
        for c in range(3):
            for i in range(16):
                out[member, c * 16 + i, :width] = total[modes[member * 16 + i]]
    return out


def split(x):
    hi = x.astype(BF16)
    return hi, (x - hi.astype(F32)).astype(BF16)


def full(shape):
    return pl.BlockSpec(shape, lambda *_: (0,) * len(shape))


def vmem(n):
    return [pl.BlockSpec(memory_space=pltpu.VMEM)] * n


LIMIT = pltpu.CompilerParams(vmem_limit_bytes=40 * 2**20)


def scatter_body(flip_ref, velocity_ref, out_ref):
    flip = flip_ref[0]
    out_ref[...] = jnp.zeros_like(out_ref)
    for q in range(4):
        y = q + flip * (3 - 2 * q)
        for j in range(OWN):
            lanes = slice((q * OWN + j) * BLK, (q * OWN + j + 1) * BLK)
            for c in range(3):
                for m in range(2):
                    row = (c * 2 + m) * 2
                    out_ref[y * TEAM + j, row : row + 2, :] = velocity_ref[c, m, :, lanes]


def scatter(flip, velocity):
    return pl.pallas_call(
        scatter_body,
        out_shape=jax.ShapeDtypeStruct((4 * TEAM, 16, BLK), F32),
        in_specs=[pl.BlockSpec(memory_space=pltpu.SMEM)] + vmem(1),
        out_specs=vmem(1)[0],
        compiler_params=LIMIT,
        name="scatter",
    )(flip, velocity)


def nonlinear_core(state, inverse_ref, derivative_ref, forward_ref):
    hi, lo = split(state)
    physical = jnp.dot(inverse_ref[...], jnp.concatenate([hi, lo, hi], axis=0), preferred_element_type=F32)
    field = [physical[:, c * BLK : (c + 1) * BLK] for c in range(3)]
    products = {pair: field[pair[0]] * field[pair[1]] for pair in PAIRS}

    def product(a, b):
        return products[(min(a, b), max(a, b))]

    left = jnp.concatenate([jnp.concatenate([product(a, 0), product(a, 1)], axis=1) for a in range(3)], axis=0)
    left_hi, left_lo = split(left)
    der_hi, der_lo = split(derivative_ref[...])
    planar = jnp.dot(
        jnp.concatenate([left_hi, left_lo], axis=0),
        jnp.concatenate([der_hi, der_lo], axis=1),
        preferred_element_type=F32,
    )
    rows = 3 * POINTS
    planar = planar[:rows, :BLK] + planar[:rows, BLK:] + planar[rows:, :BLK]
    right = jnp.concatenate(
        [jnp.concatenate([planar[a * POINTS : (a + 1) * POINTS], product(a, 2)], axis=0) for a in range(3)], axis=1
    )
    right_hi, right_lo = split(right)
    first = jnp.dot(forward_ref[...], right_hi, preferred_element_type=F32)
    second = jnp.dot(forward_ref[:POINTS, :], right_lo, preferred_element_type=F32)
    return state + (first[:POINTS] + first[POINTS:] + second)


def store_chunks(right_side, out_ref):
    for j in range(TEAM):
        for c in range(3):
            out_ref[j, c * 16 : (c + 1) * 16, :] = right_side[j * 16 : (j + 1) * 16, c * BLK : (c + 1) * BLK]


def first_body(chunks_ref, inverse_ref, derivative_ref, forward_ref, out_ref, state_ref):
    for device in range(4 * TEAM):
        y, member = divmod(device, TEAM)
        row = member * 16 + y * 4
        for c in range(3):
            state_ref[row : row + 4, c * BLK : (c + 1) * BLK] = chunks_ref[device, c * 4 : (c + 1) * 4, :]
    store_chunks(nonlinear_core(state_ref[...], inverse_ref, derivative_ref, forward_ref), out_ref)


def later_body(chunks_ref, inverse_ref, derivative_ref, forward_ref, out_ref):
    state = jnp.concatenate(
        [
            jnp.concatenate([chunks_ref[j, c * 16 : (c + 1) * 16, :] for j in range(TEAM)], axis=0)
            for c in range(3)
        ],
        axis=1,
    )
    store_chunks(nonlinear_core(state, inverse_ref, derivative_ref, forward_ref), out_ref)


def nonlinear(chunks, inverse, derivative, forward, first):
    return pl.pallas_call(
        first_body if first else later_body,
        out_shape=jax.ShapeDtypeStruct((TEAM, VEC, BLK), F32),
        in_specs=vmem(4),
        out_specs=vmem(1)[0],
        scratch_shapes=[pltpu.VMEM((POINTS, 3 * BLK), F32)] if first else [],
        compiler_params=LIMIT,
        name="nonlinear",
    )(chunks, inverse, derivative, forward)


def band_rows(near_ref, blocks_ref, row, centre, acc_ref):
    acc_ref[...] = jnp.zeros_like(acc_ref)
    for slot in range(9):
        offset = near_ref[row * 9 + slot] - centre + HW
        acc_ref[offset] += blocks_ref[0, slot]


def edge_body(near_ref, info_ref, blocks_ref, out_ref, acc_ref):
    row = info_ref[1] + pl.program_id(0)
    band_rows(near_ref, blocks_ref, row, info_ref[0] + row, acc_ref)
    out_ref[0] = acc_ref[...]


def edge_band(near, info, blocks):
    return pl.pallas_call(
        edge_body,
        out_shape=jax.ShapeDtypeStruct((EDGE, BAND, BLK, BLK), F32),
        grid_spec=pltpu.PrefetchScalarGridSpec(
            num_scalar_prefetch=2,
            grid=(EDGE,),
            in_specs=[pl.BlockSpec((1, 9, BLK, BLK), lambda i, near, info: (info[1] + i, 0, 0, 0))],
            out_specs=pl.BlockSpec((1, BAND, BLK, BLK), lambda i, near, info: (i, 0, 0, 0)),
            scratch_shapes=[pltpu.VMEM((BAND, BLK, BLK), F32)],
        ),
        compiler_params=LIMIT,
        name="edge_band",
    )(near, info, blocks)


def weight_body(near_ref, info_ref, blocks_ref, edge_ref, out_ref, acc_ref):
    row = info_ref[2] + pl.program_id(0)
    inside = jnp.logical_and(row >= 0, row < LOCAL)

    @pl.when(inside)
    def _():
        band_rows(near_ref, blocks_ref, row, info_ref[0] + row, acc_ref)

    @pl.when(jnp.logical_not(inside))
    def _():
        acc_ref[...] = edge_ref[0]

    for offset in range(BAND):
        hi, lo = split(acc_ref[offset].T)
        out_ref[0, offset * BLK : (offset + 1) * BLK, :BLK] = hi
        out_ref[0, offset * BLK : (offset + 1) * BLK, BLK:] = lo


def weights_of(near, info, blocks, edge):
    return pl.pallas_call(
        weight_body,
        out_shape=jax.ShapeDtypeStruct((ROWS, BAND * BLK, 2 * BLK), BF16),
        grid_spec=pltpu.PrefetchScalarGridSpec(
            num_scalar_prefetch=2,
            grid=(ROWS,),
            in_specs=[
                pl.BlockSpec(
                    (1, 9, BLK, BLK), lambda i, near, info: (jnp.clip(info[2] + i, 0, LOCAL - 1), 0, 0, 0)
                ),
                pl.BlockSpec(
                    (1, BAND, BLK, BLK),
                    lambda i, near, info: (
                        jnp.where(
                            info[2] + i < 0, info[2] + i + EDGE, jnp.clip(info[2] + i - LOCAL, 0, EDGE - 1)
                        ),
                        0,
                        0,
                        0,
                    ),
                ),
            ],
            out_specs=pl.BlockSpec((1, BAND * BLK, 2 * BLK), lambda i, near, info: (i, 0, 0)),
            scratch_shapes=[pltpu.VMEM((BAND, BLK, BLK), F32)],
        ),
        compiler_params=LIMIT,
        name="weights",
    )(near, info, blocks, edge)


def solve_values(own_ref, left_ref, right_ref, weight_ref, coef_ref):
    def window(w):
        if w < OWN:
            return left_ref[w]
        return own_ref[w - OWN] if w < 2 * OWN else right_ref[w - 2 * OWN]

    def stacked(x):
        return jnp.concatenate(split(x), axis=0)

    def apply(parts, rows):
        out = {}
        for w in rows:
            lhs = jnp.concatenate([parts[w + o] for o in range(-HW, HW + 1)], axis=1)
            both = jnp.dot(lhs, weight_ref[w - HW], preferred_element_type=F32)
            out[w] = both[:VEC, :BLK] + both[:VEC, BLK:] + both[VEC:, :BLK]
        return out

    one = apply({w: stacked(window(w)) for w in range(WIN)}, range(HW, WIN - HW))
    two = apply({w: stacked(x) for w, x in one.items()}, range(2 * HW, WIN - 2 * HW))
    three = apply({w: stacked(x) for w, x in two.items()}, range(3 * HW, WIN - 3 * HW))
    coef = [coef_ref[:, i : i + 1] for i in range(SWEEPS + 1)]
    return [
        coef[0] * window(w) + coef[1] * one[w] + coef[2] * two[w] + coef[3] * three[w]
        for w in range(OWN, 2 * OWN)
    ]


def solve_body(own_ref, left_ref, right_ref, weight_ref, coef_ref, out_ref):
    for j, x in enumerate(solve_values(own_ref, left_ref, right_ref, weight_ref, coef_ref)):
        out_ref[j] = x
    out_ref[OWN:] = jnp.zeros((TEAM - OWN, VEC, BLK), F32)


def last_body(own_ref, left_ref, right_ref, weight_ref, coef_ref, out_ref):
    for j, x in enumerate(solve_values(own_ref, left_ref, right_ref, weight_ref, coef_ref)):
        for y in range(4):
            for c in range(3):
                out_ref[y, j, c * 4 : (c + 1) * 4, :] = x[c * 16 + y * 4 : c * 16 + y * 4 + 4]
            out_ref[y, j, 12:, :] = jnp.zeros((4, BLK), F32)


def solve(own, left, right, weights, coef, last):
    shape = (4, OWN, 16, BLK) if last else (TEAM, VEC, BLK)
    return pl.pallas_call(
        last_body if last else solve_body,
        out_shape=jax.ShapeDtypeStruct(shape, F32),
        in_specs=vmem(5),
        out_specs=vmem(1)[0],
        compiler_params=LIMIT,
        name="solve",
    )(own, left, right, weights, coef)


def gather_body(flip_ref, chunks_ref, out_ref):
    flip = flip_ref[0]
    for q in range(4):
        y = q + flip * (3 - 2 * q)
        for j in range(OWN):
            lanes = slice((q * OWN + j) * BLK, (q * OWN + j + 1) * BLK)
            for c in range(3):
                for m in range(2):
                    row = (c * 2 + m) * 2
                    out_ref[c, m, :, lanes] = chunks_ref[y, j, row : row + 2, :]


def gather(flip, chunks):
    return pl.pallas_call(
        gather_body,
        out_shape=jax.ShapeDtypeStruct((3, 2, 2, LOCAL * BLK), F32),
        in_specs=[pl.BlockSpec(memory_space=pltpu.SMEM)] + vmem(1),
        out_specs=vmem(1)[0],
        compiler_params=LIMIT,
        name="gather",
    )(flip, chunks)


def on_device(velocity, blocks, neighbours, element_derivative):
    y, z, xl, xh, co = (lax.axis_index(axis) for axis in AXES)
    part = xh * 2 + co
    q = y + co * (3 - 2 * y)
    flip = co.reshape(1)
    info = jnp.stack([part * LOCAL, jnp.where(q < 2, 0, LOCAL - EDGE), q * OWN - EDGE]).astype(jnp.int32)
    near = neighbours.reshape(-1)
    inverse_np, forward_np = tables()
    inverse, forward = jnp.asarray(inverse_np), jnp.asarray(forward_np)
    coef = lax.dynamic_index_in_dim(jnp.asarray(solve_coefficients()), z * 2 + xl, 0, keepdims=False)
    count = BLK // ELEM
    eye = jnp.eye(count, dtype=F32)
    derivative = (
        eye[None, :, None, :, None] * element_derivative.transpose(0, 2, 1)[:, None, :, None, :]
    ).reshape(2 * BLK, BLK)

    edge = lax.ppermute(edge_band(near, info, blocks), AXES, seam_pairs())
    chunks = lax.all_to_all(scatter(flip, velocity), ("y", "z", "xl"), 0, 0, tiled=True)
    weights = None
    for step in range(STEPS):
        right_side = nonlinear(chunks, inverse, derivative, forward, step == 0)
        own = lax.all_to_all(right_side, ("z", "xl"), 0, 0, tiled=True)
        if weights is None:
            weights = weights_of(near, info, blocks, edge)
        mine = own[:OWN]
        left = lax.ppermute(mine, AXES, shift_pairs(1))
        right = lax.ppermute(mine, AXES, shift_pairs(-1))
        last = step == STEPS - 1
        chunks = solve(own, left, right, weights, coef, last)
        if not last:
            chunks = lax.all_to_all(chunks, ("z", "xl"), 0, 0, tiled=True)
    return gather(flip, lax.all_to_all(chunks, ("y",), 0, 0, tiled=True))


def solution(mesh):
    fine = Mesh(mesh.devices.reshape(4, 4, 2, 2, 2), AXES)
    field = P(None, ("y", "z", "xl"), None, ("xh", "co"))
    in_specs = (field, P(("xh", "co"), None, None, None), P(("xh", "co"), None), P())
    return jax.shard_map(on_device, mesh=fine, in_specs=in_specs, out_specs=field, check_vma=False)
```

time: 755 us -> 200 us (0.26); the launches traced: 745 us -> 198 us
  matrix products: 257 us -> 0 us
  local copies, waits for them, and re-layouts: 204 us -> 3.94 us
  waiting for transfers between devices: 78.3 us -> 31.3 us
  starting transfers between devices: 91 us -> 51.5 us
  Pallas kernels: 0 us -> 26.7 us
  blocking collectives: 97.9 us -> 83 us
  other arithmetic: 13.1 us -> 1.22 us
    dot_general x55 -> x0, matrix products: 257 us -> none  [the longest x15 229 us: apply_coupling(): coupled = jnp.einsum('cnjq,njpq->cnp', picked, blocks, precision=PRECISE)]
    unnamed x17 -> x9, local copies, waits for them, and re-layouts: 106 us -> 0.79 us
    ppermute x30 -> x11, waiting for transfers between devices: 62.2 us -> 20.2 us  [the longest x5 18.5 us: on_device(): right = lax.ppermute(mine, AXES, shift_pairs(-1))]
    all_to_all x11 -> x0, local copies, waits for them, and re-layouts: 39.8 us -> none  [the longest x6 39.4 us: on_device(): lax.all_to_all(state, 'modes', split_axis=3, concat_axis=1, tiled=True)]
    ppermute x30 -> x11, starting transfers between devices: 76.7 us -> 45.4 us  [the longest x5 29.7 us: on_device(): left = lax.ppermute(mine, AXES, shift_pairs(1))]
    add x34 -> x0, local copies, waits for them, and re-layouts: 31 us -> none  [the longest x4 24.5 us: chebyshev(): return solution + direction]
    pallas_call x0 -> x14, Pallas kernels: none -> 26.7 us  [the longest x5 9.3 us: solve(): pl.pallas_call(last_body if last else solve_body, out_shape=jax.ShapeDtyp...]
    all_to_all x8 -> x10, blocking collectives: 97.9 us -> 83 us  [the longest x5 42.2 us: on_device(): own = lax.all_to_all(right_side, ('z', 'xl'), 0, 0, tiled=True)]
  transfers between devices with their start and end apart: 32 -> 12, of which waited for: 17 -> 9; matrix products, arithmetic and copies ran while one was open for 0% -> 2% of each run, Pallas kernels for 0% -> 5%
where the time goes in v1:
time: 200 us; the launch traced here: 198 us
  blocking collectives  83 us (42%)
  starting transfers between devices  51.5 us (26%)
  waiting for transfers between devices  31.3 us (16%)
  Pallas kernels  26.7 us (13%)
  local copies, waits for them, and re-layouts  3.94 us (2%)
    all_to_all x5, blocking collectives, on_device(): own = lax.all_to_all(right_side, ('z', 'xl'), 0, 0, tiled=True)  42.2 us
    all_to_all x4, blocking collectives, on_device(): chunks = lax.all_to_all(chunks, ('z', 'xl'), 0, 0, tiled=True)  33.3 us
    ppermute x5, starting transfers between devices, on_device(): left = lax.ppermute(mine, AXES, shift_pairs(1))  29.7 us
    ppermute x5, waiting for transfers between devices, on_device(): right = lax.ppermute(mine, AXES, shift_pairs(-1))  18.5 us
    all_to_all x1, waiting for transfers between devices, on_device(): lax.all_to_all(scatter(flip, velocity), ('y', 'z', 'xl'), 0, 0, tiled=True)  11.1 us
    ppermute x5, starting transfers between devices, on_device(): right = lax.ppermute(mine, AXES, shift_pairs(-1))  9.6 us
    pallas_call x5, Pallas kernels, solve(): pl.pallas_call(last_body if last else solve_body, out_shape=jax.ShapeDtyp...  9.3 us
    pallas_call x1, Pallas kernels, weights_of(): pl.pallas_call(weight_body, out_shape=jax.ShapeDtypeStruct((ROWS, BAND *...  8.54 us
  transfers between devices with their start and end apart: 12, of which 9 were waited for; matrix products, arithmetic and copies ran while one was open for 2% of the time, Pallas kernels for 5%

profile of v1, /device:TPU:1, one launch (start us, length us, event | category | flops | bytes accessed | tf_op | source)
XLA Modules:
  0.0 198.0 jit_solution(10308314630595859769)
XLA Ops:
  1.0 3.2 %edge_band.1 = f32[4,5,128,128]{3,2,1,0:T(8,128)S(1)} custom-call(s32[216]{0:T(256)S(1)} %reshape.20.near_ref, s32[3]{0:T(128)S(1)} %pad_add_fusion.info_ref, f32[24,9,128,128]{3,2,1,0:T(8,128)} %blocks_ref.3), custom_call_target="tpu_custom_call" | custom-call | tf_op jit(solution)/shard_map/edge_band/pallas_call | solution.py:249
  4.1 6.0 %collective-permute-start.2 = (f32[4,5,128,128]{3,2,1,0:T(8,128)S(1)}, f32[4,5,128,128]{3,2,1,0:T(8,128)S(1)}, u32[]{:S(2)}, u32[]{:S(2)}) collective-permute-start(f32[4,5,128,128]{3,2,1,0:T(8,128)S(1)} %edge_band.1), channel_id=1, source_target_pairs={{96,97},{97,96},{100,101},{101,100},{104,105},{105,104},{108,109},... | collective-permute-start | bytes 3932168 | tf_op jit(solution)/shard_map/ppermute | solution.py:405
  11.0 6.2 %all-to-all-start = ((f32[32,16,128]{2,1,0:T(8,128)}), f32[32,16,128]{2,1,0:T(8,128)S(1)}, u32[]{:S(2)}, u32[]{:S(2)}) async-start(f32[32,16,128]{2,1,0:T(8,128)} %scatter.1), calls=%async_computation | async-start | bytes 524288 | tf_op jit(solution)/shard_map/all_to_all | solution.py:406
  19.9 11.1 %all-to-all-done.chunks_ref = f32[32,16,128]{2,1,0:T(8,128)S(1)} async-done(((f32[32,16,128]{2,1,0:T(8,128)}), f32[32,16,128]{2,1,0:T(8,128)S(1)}, u32[]{:S(2)}, u32[]{:S(2)}) %all-to-all-start) | async-done | bytes 262176 | tf_op jit(solution)/shard_map/all_to_all | solution.py:406
  31.9 9.4 %all_to_all.55.own_ref = f32[8,48,128]{2,1,0:T(8,128)S(1)} all-to-all(f32[8,48,128]{2,1,0:T(8,128)S(1)} %nonlinear.5), channel_id=1, replica_groups=mesh['y'=4,'z'=4,'xl'=2,'xh'=2,'co'=2] {'z','xl'}, dimensions={0} | all-to-all | bytes 393216 | tf_op jit(solution)/shard_map/all_to_all | solution.py:410
  42.0 4.2 %collective-permute-start = (f32[6,48,128]{2,1,0:T(8,128)}, f32[6,48,128]{2,1,0:T(8,128)S(1)}, u32[]{:S(2)}, u32[]{:S(2)}) collective-permute-start(f32[6,48,128]{2,1,0:T(8,128)} %slice.20), channel_id=1, source_target_pairs={{0,32},{4,36},{8,40},{12,44},{16,48},{20,52},{24,56},{28,60},{32,6... | collective-permute-start | bytes 442376 | tf_op jit(solution)/shard_map/ppermute | solution.py:414
  48.9 8.5 %weights.1.weight_ref = bf16[14,640,256]{2,1,0:T(8,128)(2,1)S(1)} custom-call(s32[216]{0:T(256)S(1)} %reshape.20.near_ref, s32[3]{0:T(128)S(1)} %pad_add_fusion.info_ref, f32[24,9,128,128]{3,2,1,0:T(8,128)} %blocks_ref.3, f32[4,5,128,128]{3,2,1,0:T(8,128)S(1)} %collective-permute-done.2.edge_ref), custom_call_target="tpu_custom_call" | custom-call | tf_op jit(solution)/shard_map/weights/pallas_call | solution.py:283
  59.3 8.2 %all_to_all.56.chunks_ref = f32[8,48,128]{2,1,0:T(8,128)S(1)} all-to-all(f32[8,48,128]{2,1,0:T(8,128)S(1)} %solve.5), channel_id=1, replica_groups=mesh['y'=4,'z'=4,'xl'=2,'xh'=2,'co'=2] {'z','xl'}, dimensions={0} | all-to-all | bytes 393216 | tf_op jit(solution)/shard_map/all_to_all | solution.py:419
  68.3 8.2 %all_to_all.57.own_ref = f32[8,48,128]{2,1,0:T(8,128)S(1)} all-to-all(f32[8,48,128]{2,1,0:T(8,128)S(1)} %nonlinear.6), channel_id=1, replica_groups=mesh['y'=4,'z'=4,'xl'=2,'xh'=2,'co'=2] {'z','xl'}, dimensions={0} | all-to-all | bytes 393216 | tf_op jit(solution)/shard_map/all_to_all | solution.py:410
  76.6 9.3 %collective-permute-start.3 = (f32[6,48,128]{2,1,0:T(8,128)S(1)}, f32[6,48,128]{2,1,0:T(8,128)S(1)}, u32[]{:S(2)}, u32[]{:S(2)}) collective-permute-start(f32[6,48,128]{2,1,0:T(8,128)S(1)} %slice.21), channel_id=1, source_target_pairs={{0,32},{4,36},{8,40},{12,44},{16,48},{20,52},{24,56},{28,60},{32,6... | collective-permute-start | bytes 442376 | tf_op jit(solution)/shard_map/ppermute | solution.py:414
  85.9 1.9 collective-permute-start.4
  88.0 5.9 %collective-permute-done.4.right_ref = f32[6,48,128]{2,1,0:T(8,128)S(1)} collective-permute-done((f32[6,48,128]{2,1,0:T(8,128)S(1)}, f32[6,48,128]{2,1,0:T(8,128)S(1)}, u32[]{:S(2)}, u32[]{:S(2)}) %collective-permute-start.4) | collective-permute-done | bytes 147488 | tf_op jit(solution)/shard_map/ppermute | solution.py:415
  95.7 8.2 %all_to_all.58.chunks_ref = f32[8,48,128]{2,1,0:T(8,128)S(1)} all-to-all(f32[8,48,128]{2,1,0:T(8,128)S(1)} %solve.6), channel_id=1, replica_groups=mesh['y'=4,'z'=4,'xl'=2,'xh'=2,'co'=2] {'z','xl'}, dimensions={0} | all-to-all | bytes 393216 | tf_op jit(solution)/shard_map/all_to_all | solution.py:419
  104.8 8.2 %all_to_all.59.own_ref = f32[8,48,128]{2,1,0:T(8,128)S(1)} all-to-all(f32[8,48,128]{2,1,0:T(8,128)S(1)} %nonlinear.7), channel_id=1, replica_groups=mesh['y'=4,'z'=4,'xl'=2,'xh'=2,'co'=2] {'z','xl'}, dimensions={0} | all-to-all | bytes 393216 | tf_op jit(solution)/shard_map/all_to_all | solution.py:410
  113.0 5.5 %collective-permute-start.5 = (f32[6,48,128]{2,1,0:T(8,128)S(1)}, f32[6,48,128]{2,1,0:T(8,128)S(1)}, u32[]{:S(2)}, u32[]{:S(2)}) collective-permute-start(f32[6,48,128]{2,1,0:T(8,128)S(1)} %slice.22), channel_id=1, source_target_pairs={{0,32},{4,36},{8,40},{12,44},{16,48},{20,52},{24,56},{28,60},{32,6... | collective-permute-start | bytes 442376 | tf_op jit(solution)/shard_map/ppermute | solution.py:414
  120.6 5.9 %collective-permute-done.6.right_ref = f32[6,48,128]{2,1,0:T(8,128)S(1)} collective-permute-done((f32[6,48,128]{2,1,0:T(8,128)S(1)}, f32[6,48,128]{2,1,0:T(8,128)S(1)}, u32[]{:S(2)}, u32[]{:S(2)}) %collective-permute-start.6) | collective-permute-done | bytes 147488 | tf_op jit(solution)/shard_map/ppermute | solution.py:415
  128.3 8.6 %all_to_all.60.chunks_ref = f32[8,48,128]{2,1,0:T(8,128)S(1)} all-to-all(f32[8,48,128]{2,1,0:T(8,128)S(1)} %solve.7), channel_id=1, replica_groups=mesh['y'=4,'z'=4,'xl'=2,'xh'=2,'co'=2] {'z','xl'}, dimensions={0} | all-to-all | bytes 393216 | tf_op jit(solution)/shard_map/all_to_all | solution.py:419
  137.8 8.2 %all_to_all.61.own_ref = f32[8,48,128]{2,1,0:T(8,128)S(1)} all-to-all(f32[8,48,128]{2,1,0:T(8,128)S(1)} %nonlinear.8), channel_id=1, replica_groups=mesh['y'=4,'z'=4,'xl'=2,'xh'=2,'co'=2] {'z','xl'}, dimensions={0} | all-to-all | bytes 393216 | tf_op jit(solution)/shard_map/all_to_all | solution.py:410
  146.0 5.5 %collective-permute-start.7 = (f32[6,48,128]{2,1,0:T(8,128)S(1)}, f32[6,48,128]{2,1,0:T(8,128)S(1)}, u32[]{:S(2)}, u32[]{:S(2)}) collective-permute-start(f32[6,48,128]{2,1,0:T(8,128)S(1)} %slice.23), channel_id=1, source_target_pairs={{0,32},{4,36},{8,40},{12,44},{16,48},{20,52},{24,56},{28,60},{32,6... | collective-permute-start | bytes 442376 | tf_op jit(solution)/shard_map/ppermute | solution.py:414
  153.7 5.9 %collective-permute-done.8.right_ref = f32[6,48,128]{2,1,0:T(8,128)S(1)} collective-permute-done((f32[6,48,128]{2,1,0:T(8,128)S(1)}, f32[6,48,128]{2,1,0:T(8,128)S(1)}, u32[]{:S(2)}, u32[]{:S(2)}) %collective-permute-start.8) | collective-permute-done | bytes 147488 | tf_op jit(solution)/shard_map/ppermute | solution.py:415
  161.4 8.2 %all_to_all.62.chunks_ref = f32[8,48,128]{2,1,0:T(8,128)S(1)} all-to-all(f32[8,48,128]{2,1,0:T(8,128)S(1)} %solve.8), channel_id=1, replica_groups=mesh['y'=4,'z'=4,'xl'=2,'xh'=2,'co'=2] {'z','xl'}, dimensions={0} | all-to-all | bytes 393216 | tf_op jit(solution)/shard_map/all_to_all | solution.py:419
  170.4 8.2 %all_to_all.63.own_ref = f32[8,48,128]{2,1,0:T(8,128)S(1)} all-to-all(f32[8,48,128]{2,1,0:T(8,128)S(1)} %nonlinear.9), channel_id=1, replica_groups=mesh['y'=4,'z'=4,'xl'=2,'xh'=2,'co'=2] {'z','xl'}, dimensions={0} | all-to-all | bytes 393216 | tf_op jit(solution)/shard_map/all_to_all | solution.py:410
  180.6 5.1 %collective-permute-start.9 = (f32[6,48,128]{2,1,0:T(8,128)S(1)}, f32[6,48,128]{2,1,0:T(8,128)S(1)}, u32[]{:S(2)}, u32[]{:S(2)}) collective-permute-start(f32[6,48,128]{2,1,0:T(8,128)S(1)} %slice.24), channel_id=1, source_target_pairs={{0,32},{4,36},{8,40},{12,44},{16,48},{20,52},{24,56},{28,60},{32,6... | collective-permute-start | bytes 442376 | tf_op jit(solution)/shard_map/ppermute | solution.py:414
  189.7 7.5 %all_to_all.64.chunks_ref = f32[4,6,16,128]{3,2,1,0:T(8,128)S(1)} all-to-all(f32[4,6,16,128]{3,2,1,0:T(8,128)S(1)} %solve.9), channel_id=1, replica_groups=mesh['y'=4,'z'=4,'xl'=2,'xh'=2,'co'=2] {'y'}, dimensions={0} | all-to-all | bytes 393216 | tf_op jit(solution)/shard_map/all_to_all | solution.py:420
  (45 shorter events, 30.3 us)
Async XLA Ops:
  1.0 9.2 %copy-start.2 = (f32[3,2,2,3072]{3,2,1,0:T(2,128)S(1)}, f32[3,2,2,3072]{3,2,1,0:T(2,128)}, u32[]{:S(2)}) copy-start(f32[3,2,2,3072]{3,2,1,0:T(2,128)} %velocity_ref.1) | copy-start | bytes 442372
  1.0 16.2 %copy-start.3 = (f32[2,16,16]{2,1,0:T(8,128)S(1)}, f32[2,16,16]{2,1,0:T(8,128)}, u32[]{:S(2)}) copy-start(f32[2,16,16]{2,1,0:T(8,128)} %param.10) | copy-start | bytes 6148
  1.0 30.1 %copy-start = (bf16[256,256]{1,0:T(8,128)(2,1)S(1)}, bf16[256,256]{1,0:T(8,128)(2,1)}, u32[]{:S(2)}) copy-start(bf16[256,256]{1,0:T(8,128)(2,1)} %constant.45.clone.forward_ref) | copy-start | bytes 393220
  1.0 30.1 %copy-start.1 = (bf16[128,384]{1,0:T(8,128)(2,1)S(1)}, bf16[128,384]{1,0:T(8,128)(2,1)}, u32[]{:S(2)}) copy-start(bf16[128,384]{1,0:T(8,128)(2,1)} %constant.44.clone.inverse_ref) | copy-start | bytes 294916
  4.1 44.7 %collective-permute-start.2 = (f32[4,5,128,128]{3,2,1,0:T(8,128)S(1)}, f32[4,5,128,128]{3,2,1,0:T(8,128)S(1)}, u32[]{:S(2)}, u32[]{:S(2)}) collective-permute-start(f32[4,5,128,128]{3,2,1,0:T(8,128)S(1)} %edge_band.1), channel_id=1, source_target_pairs={{96,97},{97,96},{100,101},{101,100},{104,105},{105,104},{108,109},... | collective-permute-start | bytes 3932168 | tf_op jit(solution)/shard_map/ppermute | solution.py:405
  11.0 20.1 %all-to-all-start = ((f32[32,16,128]{2,1,0:T(8,128)}), f32[32,16,128]{2,1,0:T(8,128)S(1)}, u32[]{:S(2)}, u32[]{:S(2)}) async-start(f32[32,16,128]{2,1,0:T(8,128)} %scatter.1), calls=%async_computation | async-start | bytes 524288 | tf_op jit(solution)/shard_map/all_to_all | solution.py:406
  42.0 15.4 %collective-permute-start = (f32[6,48,128]{2,1,0:T(8,128)}, f32[6,48,128]{2,1,0:T(8,128)S(1)}, u32[]{:S(2)}, u32[]{:S(2)}) collective-permute-start(f32[6,48,128]{2,1,0:T(8,128)} %slice.20), channel_id=1, source_target_pairs={{0,32},{4,36},{8,40},{12,44},{16,48},{20,52},{24,56},{28,60},{32,6... | collective-permute-start | bytes 442376 | tf_op jit(solution)/shard_map/ppermute | solution.py:414
  46.2 11.2 %collective-permute-start.1 = (f32[6,48,128]{2,1,0:T(8,128)}, f32[6,48,128]{2,1,0:T(8,128)S(1)}, u32[]{:S(2)}, u32[]{:S(2)}) collective-permute-start(f32[6,48,128]{2,1,0:T(8,128)} %slice.20), channel_id=1, source_target_pairs={{32,0},{36,4},{40,8},{44,12},{48,16},{52,20},{56,24},{60,28},{64,3... | collective-permute-start | bytes 442376 | tf_op jit(solution)/shard_map/ppermute | solution.py:415
  76.6 11.4 %collective-permute-start.3 = (f32[6,48,128]{2,1,0:T(8,128)S(1)}, f32[6,48,128]{2,1,0:T(8,128)S(1)}, u32[]{:S(2)}, u32[]{:S(2)}) collective-permute-start(f32[6,48,128]{2,1,0:T(8,128)S(1)} %slice.21), channel_id=1, source_target_pairs={{0,32},{4,36},{8,40},{12,44},{16,48},{20,52},{24,56},{28,60},{32,6... | collective-permute-start | bytes 442376 | tf_op jit(solution)/shard_map/ppermute | solution.py:414
  85.9 8.0 %collective-permute-start.4 = (f32[6,48,128]{2,1,0:T(8,128)S(1)}, f32[6,48,128]{2,1,0:T(8,128)S(1)}, u32[]{:S(2)}, u32[]{:S(2)}) collective-permute-start(f32[6,48,128]{2,1,0:T(8,128)S(1)} %slice.21), channel_id=1, source_target_pairs={{32,0},{36,4},{40,8},{44,12},{48,16},{52,20},{56,24},{60,28},{64,3... | collective-permute-start | bytes 442376 | tf_op jit(solution)/shard_map/ppermute | solution.py:415
  113.0 7.6 %collective-permute-start.5 = (f32[6,48,128]{2,1,0:T(8,128)S(1)}, f32[6,48,128]{2,1,0:T(8,128)S(1)}, u32[]{:S(2)}, u32[]{:S(2)}) collective-permute-start(f32[6,48,128]{2,1,0:T(8,128)S(1)} %slice.22), channel_id=1, source_target_pairs={{0,32},{4,36},{8,40},{12,44},{16,48},{20,52},{24,56},{28,60},{32,6... | collective-permute-start | bytes 442376 | tf_op jit(solution)/shard_map/ppermute | solution.py:414
  118.5 8.0 %collective-permute-start.6 = (f32[6,48,128]{2,1,0:T(8,128)S(1)}, f32[6,48,128]{2,1,0:T(8,128)S(1)}, u32[]{:S(2)}, u32[]{:S(2)}) collective-permute-start(f32[6,48,128]{2,1,0:T(8,128)S(1)} %slice.22), channel_id=1, source_target_pairs={{32,0},{36,4},{40,8},{44,12},{48,16},{52,20},{56,24},{60,28},{64,3... | collective-permute-start | bytes 442376 | tf_op jit(solution)/shard_map/ppermute | solution.py:415
  146.0 7.6 %collective-permute-start.7 = (f32[6,48,128]{2,1,0:T(8,128)S(1)}, f32[6,48,128]{2,1,0:T(8,128)S(1)}, u32[]{:S(2)}, u32[]{:S(2)}) collective-permute-start(f32[6,48,128]{2,1,0:T(8,128)S(1)} %slice.23), channel_id=1, source_target_pairs={{0,32},{4,36},{8,40},{12,44},{16,48},{20,52},{24,56},{28,60},{32,6... | collective-permute-start | bytes 442376 | tf_op jit(solution)/shard_map/ppermute | solution.py:414
  151.6 8.0 %collective-permute-start.8 = (f32[6,48,128]{2,1,0:T(8,128)S(1)}, f32[6,48,128]{2,1,0:T(8,128)S(1)}, u32[]{:S(2)}, u32[]{:S(2)}) collective-permute-start(f32[6,48,128]{2,1,0:T(8,128)S(1)} %slice.23), channel_id=1, source_target_pairs={{32,0},{36,4},{40,8},{44,12},{48,16},{52,20},{56,24},{60,28},{64,3... | collective-permute-start | bytes 442376 | tf_op jit(solution)/shard_map/ppermute | solution.py:415
  178.7 8.0 %collective-permute-start.10 = (f32[6,48,128]{2,1,0:T(8,128)S(1)}, f32[6,48,128]{2,1,0:T(8,128)S(1)}, u32[]{:S(2)}, u32[]{:S(2)}) collective-permute-start(f32[6,48,128]{2,1,0:T(8,128)S(1)} %slice.24), channel_id=1, source_target_pairs={{32,0},{36,4},{40,8},{44,12},{48,16},{52,20},{56,24},{60,28},{64,3... | collective-permute-start | bytes 442376 | tf_op jit(solution)/shard_map/ppermute | solution.py:415
  180.6 7.2 %collective-permute-start.9 = (f32[6,48,128]{2,1,0:T(8,128)S(1)}, f32[6,48,128]{2,1,0:T(8,128)S(1)}, u32[]{:S(2)}, u32[]{:S(2)}) collective-permute-start(f32[6,48,128]{2,1,0:T(8,128)S(1)} %slice.24), channel_id=1, source_target_pairs={{0,32},{4,36},{8,40},{12,44},{16,48},{20,52},{24,56},{28,60},{32,6... | collective-permute-start | bytes 442376 | tf_op jit(solution)/shard_map/ppermute | solution.py:414

commit v2 on v1

--- a/solution.py
+++ b/solution.py
@@ -46,19 +46,19 @@
     return [device_of(y, z, xl, xh, co) for z in range(4) for xl in range(2)]
 
 
-def shift_pairs(step):
-    return [
-        (a, b)
-        for rank in range(16)
-        if 0 <= rank + step < 16
-        for a, b in zip(team_devices(rank), team_devices(rank + step))
-    ]
+def swap_pairs(first):
+    pairs = []
+    for rank in range(first, 15, 2):
+        for a, b in zip(team_devices(rank), team_devices(rank + 1)):
+            pairs += [(a, b), (b, a)]
+    return pairs
 
 
 def seam_pairs():
     pairs = []
     for rank in (3, 7, 11):
-        for a, b in zip(team_devices(rank), team_devices(rank + 1)):
+        for i, a in enumerate(team_devices(rank)):
+            b = team_devices(rank + 1)[i ^ 1 if rank == 7 else i]
             pairs += [(a, b), (b, a)]
     return pairs
 
@@ -139,11 +139,17 @@
     return [pl.BlockSpec(memory_space=pltpu.VMEM)] * n
 
 
-LIMIT = pltpu.CompilerParams(vmem_limit_bytes=40 * 2**20)
-
-
-def scatter_body(flip_ref, velocity_ref, out_ref):
+LIMIT = pltpu.CompilerParams(vmem_limit_bytes=12 * 2**20)
+LARGE = pltpu.CompilerParams(vmem_limit_bytes=40 * 2**20)
+
+
+def cost(flops, transferred):
+    return pl.CostEstimate(flops=flops, bytes_accessed=transferred, transcendentals=0)
+
+
+def scatter_body(flip_ref, velocity_ref, out_ref, done_ref):
     flip = flip_ref[0]
+    done_ref[...] = jnp.zeros_like(done_ref)
     out_ref[...] = jnp.zeros_like(out_ref)
     for q in range(4):
         y = q + flip * (3 - 2 * q)
@@ -158,9 +164,9 @@
 def scatter(flip, velocity):
     return pl.pallas_call(
         scatter_body,
-        out_shape=jax.ShapeDtypeStruct((4 * TEAM, 16, BLK), F32),
+        out_shape=[jax.ShapeDtypeStruct((4 * TEAM, 16, BLK), F32), jax.ShapeDtypeStruct((8, BLK), F32)],
         in_specs=[pl.BlockSpec(memory_space=pltpu.SMEM)] + vmem(1),
-        out_specs=vmem(1)[0],
+        out_specs=vmem(2),
         compiler_params=LIMIT,
         name="scatter",
     )(flip, velocity)
@@ -200,7 +206,7 @@
             out_ref[j, c * 16 : (c + 1) * 16, :] = right_side[j * 16 : (j + 1) * 16, c * BLK : (c + 1) * BLK]
 
 
-def first_body(chunks_ref, inverse_ref, derivative_ref, forward_ref, out_ref, state_ref):
+def first_body(chunks_ref, inverse_ref, derivative_ref, forward_ref, after_ref, out_ref, state_ref):
     for device in range(4 * TEAM):
         y, member = divmod(device, TEAM)
         row = member * 16 + y * 4
@@ -220,101 +226,131 @@
     store_chunks(nonlinear_core(state, inverse_ref, derivative_ref, forward_ref), out_ref)
 
 
-def nonlinear(chunks, inverse, derivative, forward, first):
+def nonlinear(chunks, inverse, derivative, forward, after=()):
+    first = len(after) > 0
     return pl.pallas_call(
         first_body if first else later_body,
         out_shape=jax.ShapeDtypeStruct((TEAM, VEC, BLK), F32),
-        in_specs=vmem(4),
+        in_specs=vmem(4) + [pl.BlockSpec(memory_space=pl.ANY)] * len(after),
         out_specs=vmem(1)[0],
         scratch_shapes=[pltpu.VMEM((POINTS, 3 * BLK), F32)] if first else [],
         compiler_params=LIMIT,
         name="nonlinear",
-    )(chunks, inverse, derivative, forward)
-
-
-def band_rows(near_ref, blocks_ref, row, centre, acc_ref):
+    )(chunks, inverse, derivative, forward, *after)
+
+
+def build_band(near_ref, block_ref, row, centre, acc_ref):
     acc_ref[...] = jnp.zeros_like(acc_ref)
     for slot in range(9):
         offset = near_ref[row * 9 + slot] - centre + HW
-        acc_ref[offset] += blocks_ref[0, slot]
-
-
-def edge_body(near_ref, info_ref, blocks_ref, out_ref, acc_ref):
-    row = info_ref[1] + pl.program_id(0)
-    band_rows(near_ref, blocks_ref, row, info_ref[0] + row, acc_ref)
-    out_ref[0] = acc_ref[...]
-
-
-def edge_band(near, info, blocks):
+        acc_ref[offset] += block_ref[slot]
+
+
+def fetch_rows(blocks_ref, rows_ref, sem_ref, first, count):
+    def copy(i):
+        row = jnp.clip(first + i, 0, LOCAL - 1)
+        return pltpu.make_async_copy(blocks_ref.at[row], rows_ref.at[i], sem_ref.at[i])
+
+    for i in range(count):
+        copy(i).start()
+    return copy
+
+
+def edge_body(near_ref, info_ref, blocks_ref, after_ref, out_ref, rows_ref, sem_ref):
+    copy = fetch_rows(blocks_ref, rows_ref, sem_ref, info_ref[1], EDGE)
+    for i in range(EDGE):
+        row = info_ref[1] + i
+        copy(i).wait()
+        build_band(near_ref, rows_ref.at[i], row, info_ref[0] + row, out_ref.at[i])
+
+
+def edge_band(near, info, blocks, after):
+    smem = pl.BlockSpec(memory_space=pltpu.SMEM)
     return pl.pallas_call(
         edge_body,
         out_shape=jax.ShapeDtypeStruct((EDGE, BAND, BLK, BLK), F32),
-        grid_spec=pltpu.PrefetchScalarGridSpec(
-            num_scalar_prefetch=2,
-            grid=(EDGE,),
-            in_specs=[pl.BlockSpec((1, 9, BLK, BLK), lambda i, near, info: (info[1] + i, 0, 0, 0))],
-            out_specs=pl.BlockSpec((1, BAND, BLK, BLK), lambda i, near, info: (i, 0, 0, 0)),
-            scratch_shapes=[pltpu.VMEM((BAND, BLK, BLK), F32)],
-        ),
+        in_specs=[smem, smem, pl.BlockSpec(memory_space=pltpu.HBM)] + vmem(1),
+        out_specs=vmem(1)[0],
+        scratch_shapes=[pltpu.VMEM((EDGE, 9, BLK, BLK), F32), pltpu.SemaphoreType.DMA((EDGE,))],
+        compiler_params=LARGE,
+        cost_estimate=cost(10**6, 6 * 10**6),
+        name="edge_band",
+    )(near, info, blocks, after)
+
+
+def store_weights(out_ref, i, offset, block):
+    hi, lo = split(block.T)
+    out_ref[i, offset * BLK : (offset + 1) * BLK, :BLK] = hi
+    out_ref[i, offset * BLK : (offset + 1) * BLK, BLK:] = lo
+
+
+def weight_body(near_ref, info_ref, blocks_ref, out_ref, done_ref, rows_ref, acc_ref, sem_ref):
+    copy = fetch_rows(blocks_ref, rows_ref, sem_ref, info_ref[2], ROWS)
+    done_ref[...] = jnp.zeros_like(done_ref)
+    for i in range(ROWS):
+        row = jnp.clip(info_ref[2] + i, 0, LOCAL - 1)
+        copy(i).wait()
+        build_band(near_ref, rows_ref.at[i], row, info_ref[0] + row, acc_ref)
+        for offset in range(BAND):
+            store_weights(out_ref, i, offset, acc_ref[offset])
+
+
+def weights_of(near, info, blocks):
+    smem = pl.BlockSpec(memory_space=pltpu.SMEM)
+    return pl.pallas_call(
+        weight_body,
+        out_shape=[
+            jax.ShapeDtypeStruct((ROWS, BAND * BLK, 2 * BLK), BF16),
+            jax.ShapeDtypeStruct((8, BLK), F32),
+        ],
+        in_specs=[smem, smem, pl.BlockSpec(memory_space=pltpu.HBM)],
+        out_specs=vmem(2),
+        scratch_shapes=[
+            pltpu.VMEM((ROWS, 9, BLK, BLK), F32),
+            pltpu.VMEM((BAND, BLK, BLK), F32),
+            pltpu.SemaphoreType.DMA((ROWS,)),
+        ],
+        compiler_params=LARGE,
+        cost_estimate=cost(10**6, 16 * 10**6),
+        name="weights",
+    )(near, info, blocks)
+
+
+def edge_weight_body(edge_ref, out_ref):
+    for i in range(EDGE):
+        for offset in range(BAND):
+            store_weights(out_ref, i, offset, edge_ref[i, offset])
+
+
+def edge_weights_of(edge):
+    return pl.pallas_call(
+        edge_weight_body,
+        out_shape=jax.ShapeDtypeStruct((EDGE, BAND * BLK, 2 * BLK), BF16),
+        in_specs=vmem(1),
+        out_specs=vmem(1)[0],
         compiler_params=LIMIT,
-        name="edge_band",
-    )(near, info, blocks)
-
-
-def weight_body(near_ref, info_ref, blocks_ref, edge_ref, out_ref, acc_ref):
-    row = info_ref[2] + pl.program_id(0)
-    inside = jnp.logical_and(row >= 0, row < LOCAL)
-
-    @pl.when(inside)
-    def _():
-        band_rows(near_ref, blocks_ref, row, info_ref[0] + row, acc_ref)
-
-    @pl.when(jnp.logical_not(inside))
-    def _():
-        acc_ref[...] = edge_ref[0]
-
-    for offset in range(BAND):
-        hi, lo = split(acc_ref[offset].T)
-        out_ref[0, offset * BLK : (offset + 1) * BLK, :BLK] = hi
-        out_ref[0, offset * BLK : (offset + 1) * BLK, BLK:] = lo
-
-
-def weights_of(near, info, blocks, edge):
-    return pl.pallas_call(
-        weight_body,
-        out_shape=jax.ShapeDtypeStruct((ROWS, BAND * BLK, 2 * BLK), BF16),
-        grid_spec=pltpu.PrefetchScalarGridSpec(
-            num_scalar_prefetch=2,
-            grid=(ROWS,),
-            in_specs=[
-                pl.BlockSpec(
-                    (1, 9, BLK, BLK), lambda i, near, info: (jnp.clip(info[2] + i, 0, LOCAL - 1), 0, 0, 0)
-                ),
-                pl.BlockSpec(
-                    (1, BAND, BLK, BLK),
-                    lambda i, near, info: (
-                        jnp.where(
-                            info[2] + i < 0, info[2] + i + EDGE, jnp.clip(info[2] + i - LOCAL, 0, EDGE - 1)
-                        ),
-                        0,
-                        0,
-                        0,
-                    ),
-                ),
-            ],
-            out_specs=pl.BlockSpec((1, BAND * BLK, 2 * BLK), lambda i, near, info: (i, 0, 0)),
-            scratch_shapes=[pltpu.VMEM((BAND, BLK, BLK), F32)],
-        ),
-        compiler_params=LIMIT,
-        name="weights",
-    )(near, info, blocks, edge)
-
-
-def solve_values(own_ref, left_ref, right_ref, weight_ref, coef_ref):
+        cost_estimate=cost(10**6, 3 * 10**6),
+        name="edge_weights",
+    )(edge)
+
+
+def solve_values(place_ref, own_ref, even_swap_ref, odd_swap_ref, weight_ref, edge_ref, coef_ref):
+    rank = place_ref[0]
+    odd = rank % 2 == 1
+
+    def weight(row):
+        if row < EDGE:
+            return jnp.where(rank == 0, edge_ref[row], weight_ref[row])
+        if row >= EDGE + OWN:
+            return jnp.where(rank == 3, edge_ref[row - EDGE - OWN], weight_ref[row])
+        return weight_ref[row]
+
     def window(w):
         if w < OWN:
-            return left_ref[w]
-        return own_ref[w - OWN] if w < 2 * OWN else right_ref[w - 2 * OWN]
+            return jnp.where(odd, even_swap_ref[w], odd_swap_ref[w])
+        if w < 2 * OWN:
+            return own_ref[w - OWN]
+        return jnp.where(odd, odd_swap_ref[w - 2 * OWN], even_swap_ref[w - 2 * OWN])
 
     def stacked(x):
         return jnp.concatenate(split(x), axis=0)
@@ -323,7 +359,7 @@
         out = {}
         for w in rows:
             lhs = jnp.concatenate([parts[w + o] for o in range(-HW, HW + 1)], axis=1)
-            both = jnp.dot(lhs, weight_ref[w - HW], preferred_element_type=F32)
+            both = jnp.dot(lhs, weight(w - HW), preferred_element_type=F32)
             out[w] = both[:VEC, :BLK] + both[:VEC, BLK:] + both[VEC:, :BLK]
         return out
 
@@ -337,30 +373,30 @@
     ]
 
 
-def solve_body(own_ref, left_ref, right_ref, weight_ref, coef_ref, out_ref):
-    for j, x in enumerate(solve_values(own_ref, left_ref, right_ref, weight_ref, coef_ref)):
+def solve_body(place_ref, own_ref, even_swap_ref, odd_swap_ref, weight_ref, edge_ref, coef_ref, out_ref):
+    for j, x in enumerate(solve_values(place_ref, own_ref, even_swap_ref, odd_swap_ref, weight_ref, edge_ref, coef_ref)):
         out_ref[j] = x
     out_ref[OWN:] = jnp.zeros((TEAM - OWN, VEC, BLK), F32)
 
 
-def last_body(own_ref, left_ref, right_ref, weight_ref, coef_ref, out_ref):
-    for j, x in enumerate(solve_values(own_ref, left_ref, right_ref, weight_ref, coef_ref)):
+def last_body(place_ref, own_ref, even_swap_ref, odd_swap_ref, weight_ref, edge_ref, coef_ref, out_ref):
+    for j, x in enumerate(solve_values(place_ref, own_ref, even_swap_ref, odd_swap_ref, weight_ref, edge_ref, coef_ref)):
         for y in range(4):
             for c in range(3):
                 out_ref[y, j, c * 4 : (c + 1) * 4, :] = x[c * 16 + y * 4 : c * 16 + y * 4 + 4]
             out_ref[y, j, 12:, :] = jnp.zeros((4, BLK), F32)
 
 
-def solve(own, left, right, weights, coef, last):
+def solve(place, own, even_swap, odd_swap, weights, edge, coef, last):
     shape = (4, OWN, 16, BLK) if last else (TEAM, VEC, BLK)
     return pl.pallas_call(
         last_body if last else solve_body,
         out_shape=jax.ShapeDtypeStruct(shape, F32),
-        in_specs=vmem(5),
+        in_specs=[pl.BlockSpec(memory_space=pltpu.SMEM)] + vmem(6),
         out_specs=vmem(1)[0],
         compiler_params=LIMIT,
         name="solve",
-    )(own, left, right, weights, coef)
+    )(place, own, even_swap, odd_swap, weights, edge, coef)
 
 
 def gather_body(flip_ref, chunks_ref, out_ref):
@@ -391,6 +427,7 @@
     part = xh * 2 + co
     q = y + co * (3 - 2 * y)
     flip = co.reshape(1)
+    place = q.reshape(1)
     info = jnp.stack([part * LOCAL, jnp.where(q < 2, 0, LOCAL - EDGE), q * OWN - EDGE]).astype(jnp.int32)
     near = neighbours.reshape(-1)
     inverse_np, forward_np = tables()
@@ -402,19 +439,20 @@
         eye[None, :, None, :, None] * element_derivative.transpose(0, 2, 1)[:, None, :, None, :]
     ).reshape(2 * BLK, BLK)
 
-    edge = lax.ppermute(edge_band(near, info, blocks), AXES, seam_pairs())
-    chunks = lax.all_to_all(scatter(flip, velocity), ("y", "z", "xl"), 0, 0, tiled=True)
-    weights = None
+    spread, sent = scatter(flip, velocity)
+    chunks = lax.all_to_all(spread, ("y", "z", "xl"), 0, 0, tiled=True)
+    edge = lax.ppermute(edge_band(near, info, blocks, sent), AXES, seam_pairs())
+    weights, built = weights_of(near, info, blocks)
     for step in range(STEPS):
-        right_side = nonlinear(chunks, inverse, derivative, forward, step == 0)
+        right_side = nonlinear(chunks, inverse, derivative, forward, (built,) if step == 0 else ())
         own = lax.all_to_all(right_side, ("z", "xl"), 0, 0, tiled=True)
-        if weights is None:
-            weights = weights_of(near, info, blocks, edge)
+        if step == 0:
+            edge_weights = edge_weights_of(edge)
         mine = own[:OWN]
-        left = lax.ppermute(mine, AXES, shift_pairs(1))
-        right = lax.ppermute(mine, AXES, shift_pairs(-1))
+        even_swap = lax.ppermute(mine, AXES, swap_pairs(0))
+        odd_swap = lax.ppermute(mine, AXES, swap_pairs(1))
         last = step == STEPS - 1
-        chunks = solve(own, left, right, weights, coef, last)
+        chunks = solve(place, own, even_swap, odd_swap, weights, edge_weights, coef, last)
         if not last:
             chunks = lax.all_to_all(chunks, ("z", "xl"), 0, 0, tiled=True)
     return gather(flip, lax.all_to_all(chunks, ("y",), 0, 0, tiled=True))

time: 200 us -> 185 us (0.925)
  starting transfers between devices: 51.5 us -> 41.6 us
  waiting for transfers between devices: 31.3 us -> 23.8 us
  local copies, waits for them, and re-layouts: 3.94 us -> 7.36 us
  blocking collectives: 83 us -> 85.2 us
  Pallas kernels: 26.7 us -> 24.5 us
    ppermute x11, starting transfers between devices: 45.4 us -> 35.1 us  [the longest x5 28.7 us: on_device(): odd_swap = lax.ppermute(mine, AXES, swap_pairs(1))]
    all_to_all x1, waiting for transfers between devices: 11.1 us -> 0.92 us  [on_device(): chunks = lax.all_to_all(spread, ('y', 'z', 'xl'), 0, 0, tiled=True)]
    unnamed x9 -> x17, local copies, waits for them, and re-layouts: 0.79 us -> 6.09 us
    pallas_call x2 -> x3, Pallas kernels: 9.33 us -> 6.53 us  [the longest x1 5.34 us: weights_of(): pl.pallas_call(weight_body, out_shape=[jax.ShapeDtypeStruct((ROWS, BAND *...]
    ppermute x11, waiting for transfers between devices: 20.2 us -> 22.9 us  [the longest x5 12.6 us: on_device(): odd_swap = lax.ppermute(mine, AXES, swap_pairs(1))]
  transfers between devices with their start and end apart: 12 -> 12, of which waited for: 9 -> 11; matrix products, arithmetic and copies ran while one was open for 2% -> 1% of each run, Pallas kernels for 5% -> 4%
where the time goes in v2:
time: 185 us; the launch traced here: 183 us
  blocking collectives  85.2 us (46%)
  starting transfers between devices  41.6 us (22%)
  Pallas kernels  24.5 us (13%)
  waiting for transfers between devices  23.8 us (13%)
  local copies, waits for them, and re-layouts  7.36 us (4%)
    all_to_all x5, blocking collectives, on_device(): own = lax.all_to_all(right_side, ('z', 'xl'), 0, 0, tiled=True)  42.8 us
    all_to_all x4, blocking collectives, on_device(): chunks = lax.all_to_all(chunks, ('z', 'xl'), 0, 0, tiled=True)  34.8 us
    ppermute x5, starting transfers between devices, on_device(): odd_swap = lax.ppermute(mine, AXES, swap_pairs(1))  28.7 us
    ppermute x5, waiting for transfers between devices, on_device(): odd_swap = lax.ppermute(mine, AXES, swap_pairs(1))  12.6 us
    ppermute x5, waiting for transfers between devices, on_device(): even_swap = lax.ppermute(mine, AXES, swap_pairs(0))  10.2 us
    pallas_call x5, Pallas kernels, solve(): pl.pallas_call(last_body if last else solve_body, out_shape=jax.ShapeDtyp...  9.77 us
    all_to_all x1, blocking collectives, on_device(): return gather(flip, lax.all_to_all(chunks, ('y',), 0, 0, tiled=True))  7.54 us
    all_to_all x1, starting transfers between devices, on_device(): chunks = lax.all_to_all(spread, ('y', 'z', 'xl'), 0, 0, tiled=True)  6.46 us
  transfers between devices with their start and end apart: 12, of which 11 were waited for; matrix products, arithmetic and copies ran while one was open for 1% of the time, Pallas kernels for 4%

profile of v2, /device:TPU:1, one launch (start us, length us, event | category | flops | bytes accessed | tf_op | source)
XLA Modules:
  0.0 182.9 jit_solution(10219514647590934075)
XLA Ops:
  2.6 3.4 %edge_band.1 = f32[4,5,128,128]{3,2,1,0:T(8,128)} custom-call(s32[216]{0:T(256)S(1)} %reshape.24.near_ref, s32[3]{0:T(128)S(1)} %pad_add_fusion.info_ref, f32[24,9,128,128]{3,2,1,0:T(8,128)} %blocks_ref.3, f32[8,128]{1,0:T(8,128)S(1)} %get-tuple-element.12.after_ref), custom_call_target="tpu_custom_call" | custom-call | flops 1000000 | bytes 6000000 | tf_op jit(solution)/shard_map/edge_band/pallas_call | solution.py:269
  6.0 5.8 %collective-permute-start.2 = (f32[4,5,128,128]{3,2,1,0:T(8,128)}, f32[4,5,128,128]{3,2,1,0:T(8,128)S(1)}, u32[]{:S(2)}, u32[]{:S(2)}) collective-permute-start(f32[4,5,128,128]{3,2,1,0:T(8,128)} %edge_band.1), channel_id=1, source_target_pairs={{96,97},{97,96},{100,101},{101,100},{104,105},{105,104},{108,109},... | collective-permute-start | bytes 3932168 | tf_op jit(solution)/shard_map/ppermute | solution.py:444
  11.8 6.5 %all-to-all-start = ((f32[32,16,128]{2,1,0:T(8,128)}), f32[32,16,128]{2,1,0:T(8,128)S(1)}, u32[]{:S(2)}, u32[]{:S(2)}) async-start(f32[32,16,128]{2,1,0:T(8,128)} %get-tuple-element.9), calls=%async_computation | async-start | bytes 524288 | tf_op jit(solution)/shard_map/all_to_all | solution.py:443
  18.9 5.3 %weights.1 = (bf16[14,640,256]{2,1,0:T(8,128)(2,1)S(1)}, f32[8,128]{1,0:T(8,128)S(1)}) custom-call(s32[216]{0:T(256)S(1)} %reshape.24.near_ref, s32[3]{0:T(128)S(1)} %pad_add_fusion.info_ref, f32[24,9,128,128]{3,2,1,0:T(8,128)} %blocks_ref.3), custom_call_target="tpu_custom_call" | custom-call | flops 1000000 | bytes 16000000 | tf_op jit(solution)/shard_map/weights/pallas_call | solution.py:300
  28.1 9.6 %all_to_all.55.own_ref = f32[8,48,128]{2,1,0:T(8,128)S(1)} all-to-all(f32[8,48,128]{2,1,0:T(8,128)S(1)} %nonlinear.5), channel_id=1, replica_groups=mesh['y'=4,'z'=4,'xl'=2,'xh'=2,'co'=2] {'z','xl'}, dimensions={0} | all-to-all | bytes 393216 | tf_op jit(solution)/shard_map/all_to_all | solution.py:448
  37.7 8.0 %collective-permute-start.1 = (f32[6,48,128]{2,1,0:T(8,128)S(1)}, f32[6,48,128]{2,1,0:T(8,128)S(1)}, u32[]{:S(2)}, u32[]{:S(2)}) collective-permute-start(f32[6,48,128]{2,1,0:T(8,128)S(1)} %slice.20), channel_id=1, source_target_pairs={{32,64},{64,32},{36,68},{68,36},{40,72},{72,40},{44,76},{76,44},{4... | collective-permute-start | bytes 442376 | tf_op jit(solution)/shard_map/ppermute | solution.py:453
  54.0 9.0 %all_to_all.56.chunks_ref = f32[8,48,128]{2,1,0:T(8,128)S(1)} all-to-all(f32[8,48,128]{2,1,0:T(8,128)S(1)} %solve.5), channel_id=1, replica_groups=mesh['y'=4,'z'=4,'xl'=2,'xh'=2,'co'=2] {'z','xl'}, dimensions={0} | all-to-all | bytes 393216 | tf_op jit(solution)/shard_map/all_to_all | solution.py:457
  63.8 8.4 %all_to_all.57.own_ref = f32[8,48,128]{2,1,0:T(8,128)S(1)} all-to-all(f32[8,48,128]{2,1,0:T(8,128)S(1)} %nonlinear.6), channel_id=1, replica_groups=mesh['y'=4,'z'=4,'xl'=2,'xh'=2,'co'=2] {'z','xl'}, dimensions={0} | all-to-all | bytes 393216 | tf_op jit(solution)/shard_map/all_to_all | solution.py:448
  72.2 5.4 %collective-permute-start.4 = (f32[6,48,128]{2,1,0:T(8,128)S(1)}, f32[6,48,128]{2,1,0:T(8,128)S(1)}, u32[]{:S(2)}, u32[]{:S(2)}) collective-permute-start(f32[6,48,128]{2,1,0:T(8,128)S(1)} %slice.21), channel_id=1, source_target_pairs={{32,64},{64,32},{36,68},{68,36},{40,72},{72,40},{44,76},{76,44},{4... | collective-permute-start | bytes 442376 | tf_op jit(solution)/shard_map/ppermute | solution.py:453
  77.8 2.7 %collective-permute-done.4.odd_swap_ref = f32[6,48,128]{2,1,0:T(8,128)S(1)} collective-permute-done((f32[6,48,128]{2,1,0:T(8,128)S(1)}, f32[6,48,128]{2,1,0:T(8,128)S(1)}, u32[]{:S(2)}, u32[]{:S(2)}) %collective-permute-start.4) | collective-permute-done | bytes 147488 | tf_op jit(solution)/shard_map/ppermute | solution.py:453
  83.7 9.1 %all_to_all.58.chunks_ref = f32[8,48,128]{2,1,0:T(8,128)S(1)} all-to-all(f32[8,48,128]{2,1,0:T(8,128)S(1)} %solve.6), channel_id=1, replica_groups=mesh['y'=4,'z'=4,'xl'=2,'xh'=2,'co'=2] {'z','xl'}, dimensions={0} | all-to-all | bytes 393216 | tf_op jit(solution)/shard_map/all_to_all | solution.py:457
  93.7 8.3 %all_to_all.59.own_ref = f32[8,48,128]{2,1,0:T(8,128)S(1)} all-to-all(f32[8,48,128]{2,1,0:T(8,128)S(1)} %nonlinear.7), channel_id=1, replica_groups=mesh['y'=4,'z'=4,'xl'=2,'xh'=2,'co'=2] {'z','xl'}, dimensions={0} | all-to-all | bytes 393216 | tf_op jit(solution)/shard_map/all_to_all | solution.py:448
  102.0 5.4 %collective-permute-start.6 = (f32[6,48,128]{2,1,0:T(8,128)S(1)}, f32[6,48,128]{2,1,0:T(8,128)S(1)}, u32[]{:S(2)}, u32[]{:S(2)}) collective-permute-start(f32[6,48,128]{2,1,0:T(8,128)S(1)} %slice.22), channel_id=1, source_target_pairs={{32,64},{64,32},{36,68},{68,36},{40,72},{72,40},{44,76},{76,44},{4... | collective-permute-start | bytes 442376 | tf_op jit(solution)/shard_map/ppermute | solution.py:453
  114.5 8.5 %all_to_all.60.chunks_ref = f32[8,48,128]{2,1,0:T(8,128)S(1)} all-to-all(f32[8,48,128]{2,1,0:T(8,128)S(1)} %solve.7), channel_id=1, replica_groups=mesh['y'=4,'z'=4,'xl'=2,'xh'=2,'co'=2] {'z','xl'}, dimensions={0} | all-to-all | bytes 393216 | tf_op jit(solution)/shard_map/all_to_all | solution.py:457
  123.8 8.2 %all_to_all.61.own_ref = f32[8,48,128]{2,1,0:T(8,128)S(1)} all-to-all(f32[8,48,128]{2,1,0:T(8,128)S(1)} %nonlinear.8), channel_id=1, replica_groups=mesh['y'=4,'z'=4,'xl'=2,'xh'=2,'co'=2] {'z','xl'}, dimensions={0} | all-to-all | bytes 393216 | tf_op jit(solution)/shard_map/all_to_all | solution.py:448
  132.0 5.1 %collective-permute-start.8 = (f32[6,48,128]{2,1,0:T(8,128)S(1)}, f32[6,48,128]{2,1,0:T(8,128)S(1)}, u32[]{:S(2)}, u32[]{:S(2)}) collective-permute-start(f32[6,48,128]{2,1,0:T(8,128)S(1)} %slice.23), channel_id=1, source_target_pairs={{32,64},{64,32},{36,68},{68,36},{40,72},{72,40},{44,76},{76,44},{4... | collective-permute-start | bytes 442376 | tf_op jit(solution)/shard_map/ppermute | solution.py:453
  137.2 2.8 %collective-permute-done.8.odd_swap_ref = f32[6,48,128]{2,1,0:T(8,128)S(1)} collective-permute-done((f32[6,48,128]{2,1,0:T(8,128)S(1)}, f32[6,48,128]{2,1,0:T(8,128)S(1)}, u32[]{:S(2)}, u32[]{:S(2)}) %collective-permute-start.8) | collective-permute-done | bytes 147488 | tf_op jit(solution)/shard_map/ppermute | solution.py:453
  140.0 2.8 %collective-permute-done.7.even_swap_ref = f32[6,48,128]{2,1,0:T(8,128)S(1)} collective-permute-done((f32[6,48,128]{2,1,0:T(8,128)S(1)}, f32[6,48,128]{2,1,0:T(8,128)S(1)}, u32[]{:S(2)}, u32[]{:S(2)}) %collective-permute-start.7) | collective-permute-done | bytes 147488 | tf_op jit(solution)/shard_map/ppermute | solution.py:452
  144.7 8.3 %all_to_all.62.chunks_ref = f32[8,48,128]{2,1,0:T(8,128)S(1)} all-to-all(f32[8,48,128]{2,1,0:T(8,128)S(1)} %solve.8), channel_id=1, replica_groups=mesh['y'=4,'z'=4,'xl'=2,'xh'=2,'co'=2] {'z','xl'}, dimensions={0} | all-to-all | bytes 393216 | tf_op jit(solution)/shard_map/all_to_all | solution.py:457
  153.9 8.2 %all_to_all.63.own_ref = f32[8,48,128]{2,1,0:T(8,128)S(1)} all-to-all(f32[8,48,128]{2,1,0:T(8,128)S(1)} %nonlinear.9), channel_id=1, replica_groups=mesh['y'=4,'z'=4,'xl'=2,'xh'=2,'co'=2] {'z','xl'}, dimensions={0} | all-to-all | bytes 393216 | tf_op jit(solution)/shard_map/all_to_all | solution.py:448
  162.1 4.8 %collective-permute-start.10 = (f32[6,48,128]{2,1,0:T(8,128)S(1)}, f32[6,48,128]{2,1,0:T(8,128)S(1)}, u32[]{:S(2)}, u32[]{:S(2)}) collective-permute-start(f32[6,48,128]{2,1,0:T(8,128)S(1)} %slice.24), channel_id=1, source_target_pairs={{32,64},{64,32},{36,68},{68,36},{40,72},{72,40},{44,76},{76,44},{4... | collective-permute-start | bytes 442376 | tf_op jit(solution)/shard_map/ppermute | solution.py:453
  167.0 3.0 %collective-permute-done.10.odd_swap_ref = f32[6,48,128]{2,1,0:T(8,128)S(1)} collective-permute-done((f32[6,48,128]{2,1,0:T(8,128)S(1)}, f32[6,48,128]{2,1,0:T(8,128)S(1)}, u32[]{:S(2)}, u32[]{:S(2)}) %collective-permute-start.10) | collective-permute-done | bytes 147488 | tf_op jit(solution)/shard_map/ppermute | solution.py:453
  170.1 2.6 %collective-permute-done.9.even_swap_ref = f32[6,48,128]{2,1,0:T(8,128)S(1)} collective-permute-done((f32[6,48,128]{2,1,0:T(8,128)S(1)}, f32[6,48,128]{2,1,0:T(8,128)S(1)}, u32[]{:S(2)}, u32[]{:S(2)}) %collective-permute-start.9) | collective-permute-done | bytes 147488 | tf_op jit(solution)/shard_map/ppermute | solution.py:452
  174.7 7.5 %all_to_all.64.chunks_ref = f32[4,6,16,128]{3,2,1,0:T(8,128)S(1)} all-to-all(f32[4,6,16,128]{3,2,1,0:T(8,128)S(1)} %solve.9), channel_id=1, replica_groups=mesh['y'=4,'z'=4,'xl'=2,'xh'=2,'co'=2] {'y'}, dimensions={0} | all-to-all | bytes 393216 | tf_op jit(solution)/shard_map/all_to_all | solution.py:458
  (55 shorter events, 33.9 us)
Async XLA Ops:
  0.9 0.9 copy-start.4
  2.6 15.6 %copy-start.5 = (f32[2,16,16]{2,1,0:T(8,128)S(1)}, f32[2,16,16]{2,1,0:T(8,128)}, u32[]{:S(2)}) copy-start(f32[2,16,16]{2,1,0:T(8,128)} %param.10) | copy-start | bytes 6148
  6.0 40.5 %collective-permute-start.2 = (f32[4,5,128,128]{3,2,1,0:T(8,128)}, f32[4,5,128,128]{3,2,1,0:T(8,128)S(1)}, u32[]{:S(2)}, u32[]{:S(2)}) collective-permute-start(f32[4,5,128,128]{3,2,1,0:T(8,128)} %edge_band.1), channel_id=1, source_target_pairs={{96,97},{97,96},{100,101},{101,100},{104,105},{105,104},{108,109},... | collective-permute-start | bytes 3932168 | tf_op jit(solution)/shard_map/ppermute | solution.py:444
  11.8 15.4 %all-to-all-start = ((f32[32,16,128]{2,1,0:T(8,128)}), f32[32,16,128]{2,1,0:T(8,128)S(1)}, u32[]{:S(2)}, u32[]{:S(2)}) async-start(f32[32,16,128]{2,1,0:T(8,128)} %get-tuple-element.9), calls=%async_computation | async-start | bytes 524288 | tf_op jit(solution)/shard_map/all_to_all | solution.py:443
  18.8 8.4 %copy-start.2 = (bf16[256,256]{1,0:T(8,128)(2,1)S(1)}, bf16[256,256]{1,0:T(8,128)(2,1)}, u32[]{:S(2)}) copy-start(bf16[256,256]{1,0:T(8,128)(2,1)} %constant.45.clone.forward_ref) | copy-start | bytes 393220
  18.8 8.4 %copy-start.3 = (bf16[128,384]{1,0:T(8,128)(2,1)S(1)}, bf16[128,384]{1,0:T(8,128)(2,1)}, u32[]{:S(2)}) copy-start(bf16[128,384]{1,0:T(8,128)(2,1)} %constant.44.clone.inverse_ref) | copy-start | bytes 294916
  24.2 2.1 %copy-start = (bf16[14,640,256]{2,1,0:T(8,128)(2,1)}, bf16[14,640,256]{2,1,0:T(8,128)(2,1)S(1)}, u32[]{:S(2)}) copy-start(bf16[14,640,256]{2,1,0:T(8,128)(2,1)S(1)} %get-tuple-element.11.weight_ref) | copy-start | bytes 13762564
  37.7 44.1 %slice-start = ((s8[4587520]{0:T(1024)(128)(4,1)}), s8[393216]{0:T(1024)(128)(4,1)S(1)}, s32[]{:S(2)}) async-start(s8[4587520]{0:T(1024)(128)(4,1)} %bitcast.10), calls=%async_computation.11 | async-start | bytes 786432
  37.7 10.8 %collective-permute-start.1 = (f32[6,48,128]{2,1,0:T(8,128)S(1)}, f32[6,48,128]{2,1,0:T(8,128)S(1)}, u32[]{:S(2)}, u32[]{:S(2)}) collective-permute-start(f32[6,48,128]{2,1,0:T(8,128)S(1)} %slice.20), channel_id=1, source_target_pairs={{32,64},{64,32},{36,68},{68,36},{40,72},{72,40},{44,76},{76,44},{4... | collective-permute-start | bytes 442376 | tf_op jit(solution)/shard_map/ppermute | solution.py:453
  45.7 4.1 %collective-permute-start = (f32[6,48,128]{2,1,0:T(8,128)S(1)}, f32[6,48,128]{2,1,0:T(8,128)S(1)}, u32[]{:S(2)}, u32[]{:S(2)}) collective-permute-start(f32[6,48,128]{2,1,0:T(8,128)S(1)} %slice.20), channel_id=1, source_target_pairs={{0,32},{32,0},{4,36},{36,4},{8,40},{40,8},{12,44},{44,12},{16,48},... | collective-permute-start | bytes 442376 | tf_op jit(solution)/shard_map/ppermute | solution.py:452
  49.8 2.3 %copy-start.1 = (bf16[14,640,256]{2,1,0:T(8,128)(2,1)S(1)}, bf16[14,640,256]{2,1,0:T(8,128)(2,1)}, u32[]{:S(2)}) copy-start(bf16[14,640,256]{2,1,0:T(8,128)(2,1)} %copy-done) | copy-start | bytes 13762564
  52.1 29.7 %slice-start.1 = ((s8[4587520]{0:T(1024)(128)(4,1)}), s8[4194304]{0:T(1024)(128)(4,1)S(1)}, s32[]{:S(2)}) async-start(s8[4587520]{0:T(1024)(128)(4,1)} %bitcast.10), calls=%async_computation.12 | async-start | bytes 8388608
  72.2 8.2 %collective-permute-start.4 = (f32[6,48,128]{2,1,0:T(8,128)S(1)}, f32[6,48,128]{2,1,0:T(8,128)S(1)}, u32[]{:S(2)}, u32[]{:S(2)}) collective-permute-start(f32[6,48,128]{2,1,0:T(8,128)S(1)} %slice.21), channel_id=1, source_target_pairs={{32,64},{64,32},{36,68},{68,36},{40,72},{72,40},{44,76},{76,44},{4... | collective-permute-start | bytes 442376 | tf_op jit(solution)/shard_map/ppermute | solution.py:453
  77.7 4.1 %collective-permute-start.3 = (f32[6,48,128]{2,1,0:T(8,128)S(1)}, f32[6,48,128]{2,1,0:T(8,128)S(1)}, u32[]{:S(2)}, u32[]{:S(2)}) collective-permute-start(f32[6,48,128]{2,1,0:T(8,128)S(1)} %slice.21), channel_id=1, source_target_pairs={{0,32},{32,0},{4,36},{36,4},{8,40},{40,8},{12,44},{44,12},{16,48},... | collective-permute-start | bytes 442376 | tf_op jit(solution)/shard_map/ppermute | solution.py:452
  102.0 8.2 %collective-permute-start.6 = (f32[6,48,128]{2,1,0:T(8,128)S(1)}, f32[6,48,128]{2,1,0:T(8,128)S(1)}, u32[]{:S(2)}, u32[]{:S(2)}) collective-permute-start(f32[6,48,128]{2,1,0:T(8,128)S(1)} %slice.22), channel_id=1, source_target_pairs={{32,64},{64,32},{36,68},{68,36},{40,72},{72,40},{44,76},{76,44},{4... | collective-permute-start | bytes 442376 | tf_op jit(solution)/shard_map/ppermute | solution.py:453
  107.4 5.1 %collective-permute-start.5 = (f32[6,48,128]{2,1,0:T(8,128)S(1)}, f32[6,48,128]{2,1,0:T(8,128)S(1)}, u32[]{:S(2)}, u32[]{:S(2)}) collective-permute-start(f32[6,48,128]{2,1,0:T(8,128)S(1)} %slice.22), channel_id=1, source_target_pairs={{0,32},{32,0},{4,36},{36,4},{8,40},{40,8},{12,44},{44,12},{16,48},... | collective-permute-start | bytes 442376 | tf_op jit(solution)/shard_map/ppermute | solution.py:452
  132.0 8.0 %collective-permute-start.8 = (f32[6,48,128]{2,1,0:T(8,128)S(1)}, f32[6,48,128]{2,1,0:T(8,128)S(1)}, u32[]{:S(2)}, u32[]{:S(2)}) collective-permute-start(f32[6,48,128]{2,1,0:T(8,128)S(1)} %slice.23), channel_id=1, source_target_pairs={{32,64},{64,32},{36,68},{68,36},{40,72},{72,40},{44,76},{76,44},{4... | collective-permute-start | bytes 442376 | tf_op jit(solution)/shard_map/ppermute | solution.py:453
  137.1 5.6 %collective-permute-start.7 = (f32[6,48,128]{2,1,0:T(8,128)S(1)}, f32[6,48,128]{2,1,0:T(8,128)S(1)}, u32[]{:S(2)}, u32[]{:S(2)}) collective-permute-start(f32[6,48,128]{2,1,0:T(8,128)S(1)} %slice.23), channel_id=1, source_target_pairs={{0,32},{32,0},{4,36},{36,4},{8,40},{40,8},{12,44},{44,12},{16,48},... | collective-permute-start | bytes 442376 | tf_op jit(solution)/shard_map/ppermute | solution.py:452
  162.1 8.0 %collective-permute-start.10 = (f32[6,48,128]{2,1,0:T(8,128)S(1)}, f32[6,48,128]{2,1,0:T(8,128)S(1)}, u32[]{:S(2)}, u32[]{:S(2)}) collective-permute-start(f32[6,48,128]{2,1,0:T(8,128)S(1)} %slice.24), channel_id=1, source_target_pairs={{32,64},{64,32},{36,68},{68,36},{40,72},{72,40},{44,76},{76,44},{4... | collective-permute-start | bytes 442376 | tf_op jit(solution)/shard_map/ppermute | solution.py:453
  166.9 5.8 %collective-permute-start.9 = (f32[6,48,128]{2,1,0:T(8,128)S(1)}, f32[6,48,128]{2,1,0:T(8,128)S(1)}, u32[]{:S(2)}, u32[]{:S(2)}) collective-permute-start(f32[6,48,128]{2,1,0:T(8,128)S(1)} %slice.24), channel_id=1, source_target_pairs={{0,32},{32,0},{4,36},{36,4},{8,40},{40,8},{12,44},{44,12},{16,48},... | collective-permute-start | bytes 442376 | tf_op jit(solution)/shard_map/ppermute | solution.py:452

commit v3 on v2

--- a/solution.py
+++ b/solution.py
@@ -206,7 +206,7 @@
             out_ref[j, c * 16 : (c + 1) * 16, :] = right_side[j * 16 : (j + 1) * 16, c * BLK : (c + 1) * BLK]
 
 
-def first_body(chunks_ref, inverse_ref, derivative_ref, forward_ref, after_ref, out_ref, state_ref):
+def first_body(chunks_ref, inverse_ref, derivative_ref, forward_ref, after_ref, out_ref, same_ref, state_ref):
     for device in range(4 * TEAM):
         y, member = divmod(device, TEAM)
         row = member * 16 + y * 4
@@ -226,23 +226,26 @@
     store_chunks(nonlinear_core(state, inverse_ref, derivative_ref, forward_ref), out_ref)
 
 
-def nonlinear(chunks, inverse, derivative, forward, after=()):
-    first = len(after) > 0
+def nonlinear(chunks, inverse, derivative, forward, held=None):
+    first = held is not None
+    out = jax.ShapeDtypeStruct((TEAM, VEC, BLK), F32)
+    anywhere = pl.BlockSpec(memory_space=pl.ANY)
     return pl.pallas_call(
         first_body if first else later_body,
-        out_shape=jax.ShapeDtypeStruct((TEAM, VEC, BLK), F32),
-        in_specs=vmem(4) + [pl.BlockSpec(memory_space=pl.ANY)] * len(after),
-        out_specs=vmem(1)[0],
+        out_shape=[out, jax.ShapeDtypeStruct(held.shape, F32)] if first else out,
+        in_specs=vmem(4) + [anywhere] * first,
+        out_specs=vmem(1) + [anywhere] if first else vmem(1)[0],
         scratch_shapes=[pltpu.VMEM((POINTS, 3 * BLK), F32)] if first else [],
+        input_output_aliases={4: 1} if first else {},
         compiler_params=LIMIT,
         name="nonlinear",
-    )(chunks, inverse, derivative, forward, *after)
+    )(chunks, inverse, derivative, forward, *([held] if first else []))
 
 
 def build_band(near_ref, block_ref, row, centre, acc_ref):
     acc_ref[...] = jnp.zeros_like(acc_ref)
     for slot in range(9):
-        offset = near_ref[row * 9 + slot] - centre + HW
+        offset = near_ref[slot, row] - centre + HW
         acc_ref[offset] += block_ref[slot]
 
 
@@ -429,7 +432,6 @@
     flip = co.reshape(1)
     place = q.reshape(1)
     info = jnp.stack([part * LOCAL, jnp.where(q < 2, 0, LOCAL - EDGE), q * OWN - EDGE]).astype(jnp.int32)
-    near = neighbours.reshape(-1)
     inverse_np, forward_np = tables()
     inverse, forward = jnp.asarray(inverse_np), jnp.asarray(forward_np)
     coef = lax.dynamic_index_in_dim(jnp.asarray(solve_coefficients()), z * 2 + xl, 0, keepdims=False)
@@ -441,10 +443,14 @@
 
     spread, sent = scatter(flip, velocity)
     chunks = lax.all_to_all(spread, ("y", "z", "xl"), 0, 0, tiled=True)
-    edge = lax.ppermute(edge_band(near, info, blocks, sent), AXES, seam_pairs())
-    weights, built = weights_of(near, info, blocks)
+    ends = edge_band(neighbours.T, info, blocks, sent)
+    weights, built = weights_of(neighbours.T, info, blocks)
     for step in range(STEPS):
-        right_side = nonlinear(chunks, inverse, derivative, forward, (built,) if step == 0 else ())
+        if step == 0:
+            right_side, ends = nonlinear(chunks, inverse, derivative, forward, ends)
+            edge = lax.ppermute(ends, AXES, seam_pairs())
+        else:
+            right_side = nonlinear(chunks, inverse, derivative, forward)
         own = lax.all_to_all(right_side, ("z", "xl"), 0, 0, tiled=True)
         if step == 0:
             edge_weights = edge_weights_of(edge)

time: 185 us -> 180 us (0.973)
  starting transfers between devices: 41.6 us -> 46 us
  local copies, waits for them, and re-layouts: 7.36 us -> 3.48 us
  waiting for transfers between devices: 23.8 us -> 20.7 us
    ppermute x5, waiting for transfers between devices: 10.2 us -> 5.03 us  [on_device(): even_swap = lax.ppermute(mine, AXES, swap_pairs(0))]
    unnamed x17 -> x8, local copies, waits for them, and re-layouts: 6.09 us -> 0.92 us
    all_to_all x1, waiting for transfers between devices: 0.92 us -> 4.77 us  [on_device(): chunks = lax.all_to_all(spread, ('y', 'z', 'xl'), 0, 0, tiled=True)]
    all_to_all x1, starting transfers between devices: 6.46 us -> 9.94 us  [on_device(): chunks = lax.all_to_all(spread, ('y', 'z', 'xl'), 0, 0, tiled=True)]
  transfers between devices with their start and end apart: 12 -> 12, of which waited for: 11 -> 9; matrix products, arithmetic and copies ran while one was open for 1% -> 2% of each run, Pallas kernels for 4% -> 5%
where the time goes in v3:
time: 180 us; the launch traced here: 179 us
  blocking collectives  84.4 us (47%)
  starting transfers between devices  46 us (26%)
  Pallas kernels  24 us (13%)
  waiting for transfers between devices  20.7 us (12%)
  local copies, waits for them, and re-layouts  3.48 us (2%)
    all_to_all x5, blocking collectives, on_device(): own = lax.all_to_all(right_side, ('z', 'xl'), 0, 0, tiled=True)  42.3 us
    all_to_all x4, blocking collectives, on_device(): chunks = lax.all_to_all(chunks, ('z', 'xl'), 0, 0, tiled=True)  33.7 us
    ppermute x5, starting transfers between devices, on_device(): odd_swap = lax.ppermute(mine, AXES, swap_pairs(1))  30.3 us
    ppermute x5, waiting for transfers between devices, on_device(): odd_swap = lax.ppermute(mine, AXES, swap_pairs(1))  10.9 us
    all_to_all x1, starting transfers between devices, on_device(): chunks = lax.all_to_all(spread, ('y', 'z', 'xl'), 0, 0, tiled=True)  9.94 us
    pallas_call x5, Pallas kernels, solve(): pl.pallas_call(last_body if last else solve_body, out_shape=jax.ShapeDtyp...  9.77 us
    all_to_all x1, blocking collectives, on_device(): return gather(flip, lax.all_to_all(chunks, ('y',), 0, 0, tiled=True))  8.34 us
    pallas_call x1, Pallas kernels, weights_of(): pl.pallas_call(weight_body, out_shape=[jax.ShapeDtypeStruct((ROWS, BAND *...  5.83 us
  transfers between devices with their start and end apart: 12, of which 9 were waited for; matrix products, arithmetic and copies ran while one was open for 2% of the time, Pallas kernels for 5%

profile of v3, /device:TPU:1, one launch (start us, length us, event | category | flops | bytes accessed | tf_op | source)
XLA Modules:
  0.0 179.1 jit_solution(17917267057723415559)
XLA Ops:
  1.7 9.9 %all-to-all-start = ((f32[32,16,128]{2,1,0:T(8,128)}), f32[32,16,128]{2,1,0:T(8,128)S(1)}, u32[]{:S(2)}, u32[]{:S(2)}) async-start(f32[32,16,128]{2,1,0:T(8,128)} %get-tuple-element.10), calls=%async_computation | async-start | bytes 524288 | tf_op jit(solution)/shard_map/all_to_all | solution.py:445
  13.0 2.4 %edge_band.1.after_ref = f32[4,5,128,128]{3,2,1,0:T(8,128)S(1)} custom-call(s32[9,24]{1,0:T(8,128)S(1)} %bitcast.11, s32[3]{0:T(128)S(1)} %pad_add_fusion.info_ref, f32[24,9,128,128]{3,2,1,0:T(8,128)} %blocks_ref.3, f32[8,128]{1,0:T(8,128)S(1)} %get-tuple-element.11.after_ref), custom_call_target="tpu_custom_call" | custom-call | flops 1000000 | bytes 6000000 | tf_op jit(solution)/shard_map/edge_band/pallas_call | solution.py:272
  15.4 4.8 %all-to-all-done.chunks_ref = f32[32,16,128]{2,1,0:T(8,128)S(1)} async-done(((f32[32,16,128]{2,1,0:T(8,128)}), f32[32,16,128]{2,1,0:T(8,128)S(1)}, u32[]{:S(2)}, u32[]{:S(2)}) %all-to-all-start) | async-done | bytes 262176 | tf_op jit(solution)/shard_map/all_to_all | solution.py:445
  21.0 5.2 %collective-permute-start.2 = (f32[4,5,128,128]{3,2,1,0:T(8,128)S(1)}, f32[4,5,128,128]{3,2,1,0:T(8,128)S(1)}, u32[]{:S(2)}, u32[]{:S(2)}) collective-permute-start(f32[4,5,128,128]{3,2,1,0:T(8,128)S(1)} %get-tuple-element.14), channel_id=1, source_target_pairs={{96,97},{97,96},{100,101},{101,100},{104,105},{105,104},{108,109},... | collective-permute-start | bytes 3932168 | tf_op jit(solution)/shard_map/ppermute | solution.py:451
  26.3 8.2 %all_to_all.55.own_ref = f32[8,48,128]{2,1,0:T(8,128)S(1)} all-to-all(f32[8,48,128]{2,1,0:T(8,128)S(1)} %get-tuple-element.12), channel_id=1, replica_groups=mesh['y'=4,'z'=4,'xl'=2,'xh'=2,'co'=2] {'z','xl'}, dimensions={0} | all-to-all | bytes 393216 | tf_op jit(solution)/shard_map/all_to_all | solution.py:454
  35.1 3.9 %collective-permute-start.1 = (f32[6,48,128]{2,1,0:T(8,128)}, f32[6,48,128]{2,1,0:T(8,128)S(1)}, u32[]{:S(2)}, u32[]{:S(2)}) collective-permute-start(f32[6,48,128]{2,1,0:T(8,128)} %slice.20), channel_id=1, source_target_pairs={{32,64},{64,32},{36,68},{68,36},{40,72},{72,40},{44,76},{76,44},{4... | collective-permute-start | bytes 442376 | tf_op jit(solution)/shard_map/ppermute | solution.py:459
  39.2 5.8 %weights.1 = (bf16[14,640,256]{2,1,0:T(8,128)(2,1)S(1)}, f32[8,128]{1,0:T(8,128)}) custom-call(s32[9,24]{1,0:T(8,128)S(1)} %bitcast.12, s32[3]{0:T(128)S(1)} %pad_add_fusion.info_ref, f32[24,9,128,128]{3,2,1,0:T(8,128)} %blocks_ref.3), custom_call_target="tpu_custom_call" | custom-call | flops 1000000 | bytes 16000000 | tf_op jit(solution)/shard_map/weights/pallas_call | solution.py:303
  48.2 9.1 %all_to_all.56.chunks_ref = f32[8,48,128]{2,1,0:T(8,128)S(1)} all-to-all(f32[8,48,128]{2,1,0:T(8,128)S(1)} %solve.5), channel_id=1, replica_groups=mesh['y'=4,'z'=4,'xl'=2,'xh'=2,'co'=2] {'z','xl'}, dimensions={0} | all-to-all | bytes 393216 | tf_op jit(solution)/shard_map/all_to_all | solution.py:463
  58.1 8.4 %all_to_all.57.own_ref = f32[8,48,128]{2,1,0:T(8,128)S(1)} all-to-all(f32[8,48,128]{2,1,0:T(8,128)S(1)} %nonlinear.6), channel_id=1, replica_groups=mesh['y'=4,'z'=4,'xl'=2,'xh'=2,'co'=2] {'z','xl'}, dimensions={0} | all-to-all | bytes 393216 | tf_op jit(solution)/shard_map/all_to_all | solution.py:454
  66.5 6.8 %collective-permute-start.4 = (f32[6,48,128]{2,1,0:T(8,128)S(1)}, f32[6,48,128]{2,1,0:T(8,128)S(1)}, u32[]{:S(2)}, u32[]{:S(2)}) collective-permute-start(f32[6,48,128]{2,1,0:T(8,128)S(1)} %slice.21), channel_id=1, source_target_pairs={{32,64},{64,32},{36,68},{68,36},{40,72},{72,40},{44,76},{76,44},{4... | collective-permute-start | bytes 442376 | tf_op jit(solution)/shard_map/ppermute | solution.py:459
  73.3 2.7 %collective-permute-done.4.odd_swap_ref = f32[6,48,128]{2,1,0:T(8,128)S(1)} collective-permute-done((f32[6,48,128]{2,1,0:T(8,128)S(1)}, f32[6,48,128]{2,1,0:T(8,128)S(1)}, u32[]{:S(2)}, u32[]{:S(2)}) %collective-permute-start.4) | collective-permute-done | bytes 147488 | tf_op jit(solution)/shard_map/ppermute | solution.py:459
  79.3 8.2 %all_to_all.58.chunks_ref = f32[8,48,128]{2,1,0:T(8,128)S(1)} all-to-all(f32[8,48,128]{2,1,0:T(8,128)S(1)} %solve.6), channel_id=1, replica_groups=mesh['y'=4,'z'=4,'xl'=2,'xh'=2,'co'=2] {'z','xl'}, dimensions={0} | all-to-all | bytes 393216 | tf_op jit(solution)/shard_map/all_to_all | solution.py:463
  88.3 8.2 %all_to_all.59.own_ref = f32[8,48,128]{2,1,0:T(8,128)S(1)} all-to-all(f32[8,48,128]{2,1,0:T(8,128)S(1)} %nonlinear.7), channel_id=1, replica_groups=mesh['y'=4,'z'=4,'xl'=2,'xh'=2,'co'=2] {'z','xl'}, dimensions={0} | all-to-all | bytes 393216 | tf_op jit(solution)/shard_map/all_to_all | solution.py:454
  96.5 6.7 %collective-permute-start.6 = (f32[6,48,128]{2,1,0:T(8,128)S(1)}, f32[6,48,128]{2,1,0:T(8,128)S(1)}, u32[]{:S(2)}, u32[]{:S(2)}) collective-permute-start(f32[6,48,128]{2,1,0:T(8,128)S(1)} %slice.22), channel_id=1, source_target_pairs={{32,64},{64,32},{36,68},{68,36},{40,72},{72,40},{44,76},{76,44},{4... | collective-permute-start | bytes 442376 | tf_op jit(solution)/shard_map/ppermute | solution.py:459
  103.5 2.7 %collective-permute-done.6.odd_swap_ref = f32[6,48,128]{2,1,0:T(8,128)S(1)} collective-permute-done((f32[6,48,128]{2,1,0:T(8,128)S(1)}, f32[6,48,128]{2,1,0:T(8,128)S(1)}, u32[]{:S(2)}, u32[]{:S(2)}) %collective-permute-start.6) | collective-permute-done | bytes 147488 | tf_op jit(solution)/shard_map/ppermute | solution.py:459
  109.5 8.2 %all_to_all.60.chunks_ref = f32[8,48,128]{2,1,0:T(8,128)S(1)} all-to-all(f32[8,48,128]{2,1,0:T(8,128)S(1)} %solve.7), channel_id=1, replica_groups=mesh['y'=4,'z'=4,'xl'=2,'xh'=2,'co'=2] {'z','xl'}, dimensions={0} | all-to-all | bytes 393216 | tf_op jit(solution)/shard_map/all_to_all | solution.py:463
  118.5 8.2 %all_to_all.61.own_ref = f32[8,48,128]{2,1,0:T(8,128)S(1)} all-to-all(f32[8,48,128]{2,1,0:T(8,128)S(1)} %nonlinear.8), channel_id=1, replica_groups=mesh['y'=4,'z'=4,'xl'=2,'xh'=2,'co'=2] {'z','xl'}, dimensions={0} | all-to-all | bytes 393216 | tf_op jit(solution)/shard_map/all_to_all | solution.py:454
  126.8 6.6 %collective-permute-start.8 = (f32[6,48,128]{2,1,0:T(8,128)S(1)}, f32[6,48,128]{2,1,0:T(8,128)S(1)}, u32[]{:S(2)}, u32[]{:S(2)}) collective-permute-start(f32[6,48,128]{2,1,0:T(8,128)S(1)} %slice.23), channel_id=1, source_target_pairs={{32,64},{64,32},{36,68},{68,36},{40,72},{72,40},{44,76},{76,44},{4... | collective-permute-start | bytes 442376 | tf_op jit(solution)/shard_map/ppermute | solution.py:459
  133.5 2.7 %collective-permute-done.8.odd_swap_ref = f32[6,48,128]{2,1,0:T(8,128)S(1)} collective-permute-done((f32[6,48,128]{2,1,0:T(8,128)S(1)}, f32[6,48,128]{2,1,0:T(8,128)S(1)}, u32[]{:S(2)}, u32[]{:S(2)}) %collective-permute-start.8) | collective-permute-done | bytes 147488 | tf_op jit(solution)/shard_map/ppermute | solution.py:459
  139.4 8.2 %all_to_all.62.chunks_ref = f32[8,48,128]{2,1,0:T(8,128)S(1)} all-to-all(f32[8,48,128]{2,1,0:T(8,128)S(1)} %solve.8), channel_id=1, replica_groups=mesh['y'=4,'z'=4,'xl'=2,'xh'=2,'co'=2] {'z','xl'}, dimensions={0} | all-to-all | bytes 393216 | tf_op jit(solution)/shard_map/all_to_all | solution.py:463
  148.4 9.3 %all_to_all.63.own_ref = f32[8,48,128]{2,1,0:T(8,128)S(1)} all-to-all(f32[8,48,128]{2,1,0:T(8,128)S(1)} %nonlinear.9), channel_id=1, replica_groups=mesh['y'=4,'z'=4,'xl'=2,'xh'=2,'co'=2] {'z','xl'}, dimensions={0} | all-to-all | bytes 393216 | tf_op jit(solution)/shard_map/all_to_all | solution.py:454
  157.8 6.2 %collective-permute-start.10 = (f32[6,48,128]{2,1,0:T(8,128)S(1)}, f32[6,48,128]{2,1,0:T(8,128)S(1)}, u32[]{:S(2)}, u32[]{:S(2)}) collective-permute-start(f32[6,48,128]{2,1,0:T(8,128)S(1)} %slice.24), channel_id=1, source_target_pairs={{32,64},{64,32},{36,68},{68,36},{40,72},{72,40},{44,76},{76,44},{4... | collective-permute-start | bytes 442376 | tf_op jit(solution)/shard_map/ppermute | solution.py:459
  164.1 2.7 %collective-permute-done.10.odd_swap_ref = f32[6,48,128]{2,1,0:T(8,128)S(1)} collective-permute-done((f32[6,48,128]{2,1,0:T(8,128)S(1)}, f32[6,48,128]{2,1,0:T(8,128)S(1)}, u32[]{:S(2)}, u32[]{:S(2)}) %collective-permute-start.10) | collective-permute-done | bytes 147488 | tf_op jit(solution)/shard_map/ppermute | solution.py:459
  170.1 8.3 %all_to_all.64.chunks_ref = f32[4,6,16,128]{3,2,1,0:T(8,128)S(1)} all-to-all(f32[4,6,16,128]{3,2,1,0:T(8,128)S(1)} %solve.9), channel_id=1, replica_groups=mesh['y'=4,'z'=4,'xl'=2,'xh'=2,'co'=2] {'y'}, dimensions={0} | all-to-all | bytes 393216 | tf_op jit(solution)/shard_map/all_to_all | solution.py:464
  (44 shorter events, 25.2 us)
Async XLA Ops:
  0.0 0.9 copy-start.2
  1.7 11.3 %copy-start.3 = (s32[24,9]{0,1:T(8,128)S(1)}, s32[24,9]{0,1:T(8,128)}, u32[]{:S(2)}) copy-start(s32[24,9]{0,1:T(8,128)} %param.9) | copy-start | bytes 2596
  1.7 18.5 %all-to-all-start = ((f32[32,16,128]{2,1,0:T(8,128)}), f32[32,16,128]{2,1,0:T(8,128)S(1)}, u32[]{:S(2)}, u32[]{:S(2)}) async-start(f32[32,16,128]{2,1,0:T(8,128)} %get-tuple-element.10), calls=%async_computation | async-start | bytes 524288 | tf_op jit(solution)/shard_map/all_to_all | solution.py:445
  13.0 7.2 %copy-start = (bf16[256,256]{1,0:T(8,128)(2,1)S(1)}, bf16[256,256]{1,0:T(8,128)(2,1)}, u32[]{:S(2)}) copy-start(bf16[256,256]{1,0:T(8,128)(2,1)} %constant.45.clone.forward_ref) | copy-start | bytes 393220
  13.0 7.2 %copy-start.1 = (bf16[128,384]{1,0:T(8,128)(2,1)S(1)}, bf16[128,384]{1,0:T(8,128)(2,1)}, u32[]{:S(2)}) copy-start(bf16[128,384]{1,0:T(8,128)(2,1)} %constant.44.clone.inverse_ref) | copy-start | bytes 294916
  21.0 24.7 %collective-permute-start.2 = (f32[4,5,128,128]{3,2,1,0:T(8,128)S(1)}, f32[4,5,128,128]{3,2,1,0:T(8,128)S(1)}, u32[]{:S(2)}, u32[]{:S(2)}) collective-permute-start(f32[4,5,128,128]{3,2,1,0:T(8,128)S(1)} %get-tuple-element.14), channel_id=1, source_target_pairs={{96,97},{97,96},{100,101},{101,100},{104,105},{105,104},{108,109},... | collective-permute-start | bytes 3932168 | tf_op jit(solution)/shard_map/ppermute | solution.py:451
  35.1 11.0 %collective-permute-start.1 = (f32[6,48,128]{2,1,0:T(8,128)}, f32[6,48,128]{2,1,0:T(8,128)S(1)}, u32[]{:S(2)}, u32[]{:S(2)}) collective-permute-start(f32[6,48,128]{2,1,0:T(8,128)} %slice.20), channel_id=1, source_target_pairs={{32,64},{64,32},{36,68},{68,36},{40,72},{72,40},{44,76},{76,44},{4... | collective-permute-start | bytes 442376 | tf_op jit(solution)/shard_map/ppermute | solution.py:459
  39.1 7.1 %collective-permute-start = (f32[6,48,128]{2,1,0:T(8,128)}, f32[6,48,128]{2,1,0:T(8,128)S(1)}, u32[]{:S(2)}, u32[]{:S(2)}) collective-permute-start(f32[6,48,128]{2,1,0:T(8,128)} %slice.20), channel_id=1, source_target_pairs={{0,32},{32,0},{4,36},{36,4},{8,40},{40,8},{12,44},{44,12},{16,48},... | collective-permute-start | bytes 442376 | tf_op jit(solution)/shard_map/ppermute | solution.py:458
  66.5 9.6 %collective-permute-start.4 = (f32[6,48,128]{2,1,0:T(8,128)S(1)}, f32[6,48,128]{2,1,0:T(8,128)S(1)}, u32[]{:S(2)}, u32[]{:S(2)}) collective-permute-start(f32[6,48,128]{2,1,0:T(8,128)S(1)} %slice.21), channel_id=1, source_target_pairs={{32,64},{64,32},{36,68},{68,36},{40,72},{72,40},{44,76},{76,44},{4... | collective-permute-start | bytes 442376 | tf_op jit(solution)/shard_map/ppermute | solution.py:459
  73.2 4.1 %collective-permute-start.3 = (f32[6,48,128]{2,1,0:T(8,128)S(1)}, f32[6,48,128]{2,1,0:T(8,128)S(1)}, u32[]{:S(2)}, u32[]{:S(2)}) collective-permute-start(f32[6,48,128]{2,1,0:T(8,128)S(1)} %slice.21), channel_id=1, source_target_pairs={{0,32},{32,0},{4,36},{36,4},{8,40},{40,8},{12,44},{44,12},{16,48},... | collective-permute-start | bytes 442376 | tf_op jit(solution)/shard_map/ppermute | solution.py:458
  96.5 9.7 %collective-permute-start.6 = (f32[6,48,128]{2,1,0:T(8,128)S(1)}, f32[6,48,128]{2,1,0:T(8,128)S(1)}, u32[]{:S(2)}, u32[]{:S(2)}) collective-permute-start(f32[6,48,128]{2,1,0:T(8,128)S(1)} %slice.22), channel_id=1, source_target_pairs={{32,64},{64,32},{36,68},{68,36},{40,72},{72,40},{44,76},{76,44},{4... | collective-permute-start | bytes 442376 | tf_op jit(solution)/shard_map/ppermute | solution.py:459
  103.3 4.3 %collective-permute-start.5 = (f32[6,48,128]{2,1,0:T(8,128)S(1)}, f32[6,48,128]{2,1,0:T(8,128)S(1)}, u32[]{:S(2)}, u32[]{:S(2)}) collective-permute-start(f32[6,48,128]{2,1,0:T(8,128)S(1)} %slice.22), channel_id=1, source_target_pairs={{0,32},{32,0},{4,36},{36,4},{8,40},{40,8},{12,44},{44,12},{16,48},... | collective-permute-start | bytes 442376 | tf_op jit(solution)/shard_map/ppermute | solution.py:458
  126.8 9.4 %collective-permute-start.8 = (f32[6,48,128]{2,1,0:T(8,128)S(1)}, f32[6,48,128]{2,1,0:T(8,128)S(1)}, u32[]{:S(2)}, u32[]{:S(2)}) collective-permute-start(f32[6,48,128]{2,1,0:T(8,128)S(1)} %slice.23), channel_id=1, source_target_pairs={{32,64},{64,32},{36,68},{68,36},{40,72},{72,40},{44,76},{76,44},{4... | collective-permute-start | bytes 442376 | tf_op jit(solution)/shard_map/ppermute | solution.py:459
  133.4 4.1 %collective-permute-start.7 = (f32[6,48,128]{2,1,0:T(8,128)S(1)}, f32[6,48,128]{2,1,0:T(8,128)S(1)}, u32[]{:S(2)}, u32[]{:S(2)}) collective-permute-start(f32[6,48,128]{2,1,0:T(8,128)S(1)} %slice.23), channel_id=1, source_target_pairs={{0,32},{32,0},{4,36},{36,4},{8,40},{40,8},{12,44},{44,12},{16,48},... | collective-permute-start | bytes 442376 | tf_op jit(solution)/shard_map/ppermute | solution.py:458
  157.8 9.1 %collective-permute-start.10 = (f32[6,48,128]{2,1,0:T(8,128)S(1)}, f32[6,48,128]{2,1,0:T(8,128)S(1)}, u32[]{:S(2)}, u32[]{:S(2)}) collective-permute-start(f32[6,48,128]{2,1,0:T(8,128)S(1)} %slice.24), channel_id=1, source_target_pairs={{32,64},{64,32},{36,68},{68,36},{40,72},{72,40},{44,76},{76,44},{4... | collective-permute-start | bytes 442376 | tf_op jit(solution)/shard_map/ppermute | solution.py:459
  164.0 4.1 %collective-permute-start.9 = (f32[6,48,128]{2,1,0:T(8,128)S(1)}, f32[6,48,128]{2,1,0:T(8,128)S(1)}, u32[]{:S(2)}, u32[]{:S(2)}) collective-permute-start(f32[6,48,128]{2,1,0:T(8,128)S(1)} %slice.24), channel_id=1, source_target_pairs={{0,32},{32,0},{4,36},{36,4},{8,40},{40,8},{12,44},{44,12},{16,48},... | collective-permute-start | bytes 442376 | tf_op jit(solution)/shard_map/ppermute | solution.py:458

commit v4 on v3

--- a/solution.py
+++ b/solution.py
@@ -140,6 +140,7 @@
 
 
 LIMIT = pltpu.CompilerParams(vmem_limit_bytes=12 * 2**20)
+MIDDLE = pltpu.CompilerParams(vmem_limit_bytes=16 * 2**20)
 LARGE = pltpu.CompilerParams(vmem_limit_bytes=40 * 2**20)
 
 
@@ -313,7 +314,7 @@
             pltpu.VMEM((BAND, BLK, BLK), F32),
             pltpu.SemaphoreType.DMA((ROWS,)),
         ],
-        compiler_params=LARGE,
+        compiler_params=MIDDLE,
         cost_estimate=cost(10**6, 16 * 10**6),
         name="weights",
     )(near, info, blocks)

time: 180 us -> 185 us (1.028)
  local copies, waits for them, and re-layouts: 3.48 us -> 8.49 us
  starting transfers between devices: 46 us -> 41.2 us
  blocking collectives: 84.4 us -> 86.7 us
    unnamed x8 -> x10, local copies, waits for them, and re-layouts: 0.92 us -> 5.94 us
    ppermute x5, starting transfers between devices: 30.3 us -> 25.6 us  [on_device(): odd_swap = lax.ppermute(mine, AXES, swap_pairs(1))]
    all_to_all x4, blocking collectives: 33.7 us -> 35.9 us  [on_device(): chunks = lax.all_to_all(chunks, ('z', 'xl'), 0, 0, tiled=True)]
where the time goes in v4:
time: 185 us; the launch traced here: 182 us
  blocking collectives  86.7 us (47%)
  starting transfers between devices  41.2 us (22%)
  Pallas kernels  24.7 us (13%)
  waiting for transfers between devices  20.7 us (11%)
  local copies, waits for them, and re-layouts  8.49 us (5%)
    all_to_all x5, blocking collectives, on_device(): own = lax.all_to_all(right_side, ('z', 'xl'), 0, 0, tiled=True)  42.9 us
    all_to_all x4, blocking collectives, on_device(): chunks = lax.all_to_all(chunks, ('z', 'xl'), 0, 0, tiled=True)  35.9 us
    ppermute x5, starting transfers between devices, on_device(): odd_swap = lax.ppermute(mine, AXES, swap_pairs(1))  25.6 us
    ppermute x5, waiting for transfers between devices, on_device(): odd_swap = lax.ppermute(mine, AXES, swap_pairs(1))  11.2 us
    all_to_all x1, starting transfers between devices, on_device(): chunks = lax.all_to_all(spread, ('y', 'z', 'xl'), 0, 0, tiled=True)  9.94 us
    pallas_call x5, Pallas kernels, solve(): pl.pallas_call(last_body if last else solve_body, out_shape=jax.ShapeDtyp...  9.77 us
    all_to_all x1, blocking collectives, on_device(): return gather(flip, lax.all_to_all(chunks, ('y',), 0, 0, tiled=True))  7.92 us
    pallas_call x1, Pallas kernels, weights_of(): pl.pallas_call(weight_body, out_shape=[jax.ShapeDtypeStruct((ROWS, BAND *...  6.49 us
  transfers between devices with their start and end apart: 12, of which 9 were waited for; matrix products, arithmetic and copies ran while one was open for 2% of the time, Pallas kernels for 5%

profile of v4, /device:TPU:1, one launch (start us, length us, event | category | flops | bytes accessed | tf_op | source)
XLA Modules:
  0.0 182.4 jit_solution(10224180545376029674)
XLA Ops:
  1.7 9.9 %all-to-all-start = ((f32[32,16,128]{2,1,0:T(8,128)}), f32[32,16,128]{2,1,0:T(8,128)S(1)}, u32[]{:S(2)}, u32[]{:S(2)}) async-start(f32[32,16,128]{2,1,0:T(8,128)} %get-tuple-element.10), calls=%async_computation | async-start | bytes 524288 | tf_op jit(solution)/shard_map/all_to_all | solution.py:446
  15.4 4.8 %all-to-all-done.chunks_ref = f32[32,16,128]{2,1,0:T(8,128)S(1)} async-done(((f32[32,16,128]{2,1,0:T(8,128)}), f32[32,16,128]{2,1,0:T(8,128)S(1)}, u32[]{:S(2)}, u32[]{:S(2)}) %all-to-all-start) | async-done | bytes 262176 | tf_op jit(solution)/shard_map/all_to_all | solution.py:446
  21.1 5.2 %collective-permute-start.2 = (f32[4,5,128,128]{3,2,1,0:T(8,128)S(1)}, f32[4,5,128,128]{3,2,1,0:T(8,128)S(1)}, u32[]{:S(2)}, u32[]{:S(2)}) collective-permute-start(f32[4,5,128,128]{3,2,1,0:T(8,128)S(1)} %get-tuple-element.14), channel_id=1, source_target_pairs={{96,97},{97,96},{100,101},{101,100},{104,105},{105,104},{108,109},... | collective-permute-start | bytes 3932168 | tf_op jit(solution)/shard_map/ppermute | solution.py:452
  26.3 8.2 %all_to_all.55.own_ref = f32[8,48,128]{2,1,0:T(8,128)S(1)} all-to-all(f32[8,48,128]{2,1,0:T(8,128)S(1)} %get-tuple-element.12), channel_id=1, replica_groups=mesh['y'=4,'z'=4,'xl'=2,'xh'=2,'co'=2] {'z','xl'}, dimensions={0} | all-to-all | bytes 393216 | tf_op jit(solution)/shard_map/all_to_all | solution.py:455
  35.2 3.9 %collective-permute-start.1 = (f32[6,48,128]{2,1,0:T(8,128)}, f32[6,48,128]{2,1,0:T(8,128)S(1)}, u32[]{:S(2)}, u32[]{:S(2)}) collective-permute-start(f32[6,48,128]{2,1,0:T(8,128)} %slice.20), channel_id=1, source_target_pairs={{32,64},{64,32},{36,68},{68,36},{40,72},{72,40},{44,76},{76,44},{4... | collective-permute-start | bytes 442376 | tf_op jit(solution)/shard_map/ppermute | solution.py:460
  39.2 5.0 %copy-done = f32[24,9,128,128]{3,2,1,0:T(8,128)S(1)} copy-done((f32[24,9,128,128]{3,2,1,0:T(8,128)S(1)}, f32[24,9,128,128]{3,2,1,0:T(8,128)}, u32[]{:S(2)}) %copy-start) | copy-done | bytes 14155800
  44.2 6.5 %weights.1 = (bf16[14,640,256]{2,1,0:T(8,128)(2,1)S(1)}, f32[8,128]{1,0:T(8,128)}) custom-call(s32[9,24]{1,0:T(8,128)S(1)} %bitcast.12, s32[3]{0:T(128)S(1)} %pad_add_fusion.info_ref, f32[24,9,128,128]{3,2,1,0:T(8,128)S(1)} %copy-done), custom_call_target="tpu_custom_call" | custom-call | flops 1000000 | bytes 16000000 | tf_op jit(solution)/shard_map/weights/pallas_call | solution.py:304
  53.9 8.2 %all_to_all.56.chunks_ref = f32[8,48,128]{2,1,0:T(8,128)S(1)} all-to-all(f32[8,48,128]{2,1,0:T(8,128)S(1)} %solve.5), channel_id=1, replica_groups=mesh['y'=4,'z'=4,'xl'=2,'xh'=2,'co'=2] {'z','xl'}, dimensions={0} | all-to-all | bytes 393216 | tf_op jit(solution)/shard_map/all_to_all | solution.py:464
  62.9 9.1 %all_to_all.57.own_ref = f32[8,48,128]{2,1,0:T(8,128)S(1)} all-to-all(f32[8,48,128]{2,1,0:T(8,128)S(1)} %nonlinear.6), channel_id=1, replica_groups=mesh['y'=4,'z'=4,'xl'=2,'xh'=2,'co'=2] {'z','xl'}, dimensions={0} | all-to-all | bytes 393216 | tf_op jit(solution)/shard_map/all_to_all | solution.py:455
  72.0 5.3 %collective-permute-start.4 = (f32[6,48,128]{2,1,0:T(8,128)S(1)}, f32[6,48,128]{2,1,0:T(8,128)S(1)}, u32[]{:S(2)}, u32[]{:S(2)}) collective-permute-start(f32[6,48,128]{2,1,0:T(8,128)S(1)} %slice.21), channel_id=1, source_target_pairs={{32,64},{64,32},{36,68},{68,36},{40,72},{72,40},{44,76},{76,44},{4... | collective-permute-start | bytes 442376 | tf_op jit(solution)/shard_map/ppermute | solution.py:460
  77.5 2.7 %collective-permute-done.4.odd_swap_ref = f32[6,48,128]{2,1,0:T(8,128)S(1)} collective-permute-done((f32[6,48,128]{2,1,0:T(8,128)S(1)}, f32[6,48,128]{2,1,0:T(8,128)S(1)}, u32[]{:S(2)}, u32[]{:S(2)}) %collective-permute-start.4) | collective-permute-done | bytes 147488 | tf_op jit(solution)/shard_map/ppermute | solution.py:460
  83.4 8.7 %all_to_all.58.chunks_ref = f32[8,48,128]{2,1,0:T(8,128)S(1)} all-to-all(f32[8,48,128]{2,1,0:T(8,128)S(1)} %solve.6), channel_id=1, replica_groups=mesh['y'=4,'z'=4,'xl'=2,'xh'=2,'co'=2] {'z','xl'}, dimensions={0} | all-to-all | bytes 393216 | tf_op jit(solution)/shard_map/all_to_all | solution.py:464
  92.9 8.5 %all_to_all.59.own_ref = f32[8,48,128]{2,1,0:T(8,128)S(1)} all-to-all(f32[8,48,128]{2,1,0:T(8,128)S(1)} %nonlinear.7), channel_id=1, replica_groups=mesh['y'=4,'z'=4,'xl'=2,'xh'=2,'co'=2] {'z','xl'}, dimensions={0} | all-to-all | bytes 393216 | tf_op jit(solution)/shard_map/all_to_all | solution.py:455
  101.4 5.6 %collective-permute-start.6 = (f32[6,48,128]{2,1,0:T(8,128)S(1)}, f32[6,48,128]{2,1,0:T(8,128)S(1)}, u32[]{:S(2)}, u32[]{:S(2)}) collective-permute-start(f32[6,48,128]{2,1,0:T(8,128)S(1)} %slice.22), channel_id=1, source_target_pairs={{32,64},{64,32},{36,68},{68,36},{40,72},{72,40},{44,76},{76,44},{4... | collective-permute-start | bytes 442376 | tf_op jit(solution)/shard_map/ppermute | solution.py:460
  107.2 2.7 %collective-permute-done.6.odd_swap_ref = f32[6,48,128]{2,1,0:T(8,128)S(1)} collective-permute-done((f32[6,48,128]{2,1,0:T(8,128)S(1)}, f32[6,48,128]{2,1,0:T(8,128)S(1)}, u32[]{:S(2)}, u32[]{:S(2)}) %collective-permute-start.6) | collective-permute-done | bytes 147488 | tf_op jit(solution)/shard_map/ppermute | solution.py:460
  113.1 9.5 %all_to_all.60.chunks_ref = f32[8,48,128]{2,1,0:T(8,128)S(1)} all-to-all(f32[8,48,128]{2,1,0:T(8,128)S(1)} %solve.7), channel_id=1, replica_groups=mesh['y'=4,'z'=4,'xl'=2,'xh'=2,'co'=2] {'z','xl'}, dimensions={0} | all-to-all | bytes 393216 | tf_op jit(solution)/shard_map/all_to_all | solution.py:464
  123.5 8.5 %all_to_all.61.own_ref = f32[8,48,128]{2,1,0:T(8,128)S(1)} all-to-all(f32[8,48,128]{2,1,0:T(8,128)S(1)} %nonlinear.8), channel_id=1, replica_groups=mesh['y'=4,'z'=4,'xl'=2,'xh'=2,'co'=2] {'z','xl'}, dimensions={0} | all-to-all | bytes 393216 | tf_op jit(solution)/shard_map/all_to_all | solution.py:455
  132.0 5.9 %collective-permute-start.8 = (f32[6,48,128]{2,1,0:T(8,128)S(1)}, f32[6,48,128]{2,1,0:T(8,128)S(1)}, u32[]{:S(2)}, u32[]{:S(2)}) collective-permute-start(f32[6,48,128]{2,1,0:T(8,128)S(1)} %slice.23), channel_id=1, source_target_pairs={{32,64},{64,32},{36,68},{68,36},{40,72},{72,40},{44,76},{76,44},{4... | collective-permute-start | bytes 442376 | tf_op jit(solution)/shard_map/ppermute | solution.py:460
  138.0 2.7 %collective-permute-done.8.odd_swap_ref = f32[6,48,128]{2,1,0:T(8,128)S(1)} collective-permute-done((f32[6,48,128]{2,1,0:T(8,128)S(1)}, f32[6,48,128]{2,1,0:T(8,128)S(1)}, u32[]{:S(2)}, u32[]{:S(2)}) %collective-permute-start.8) | collective-permute-done | bytes 147488 | tf_op jit(solution)/shard_map/ppermute | solution.py:460
  143.9 9.5 %all_to_all.62.chunks_ref = f32[8,48,128]{2,1,0:T(8,128)S(1)} all-to-all(f32[8,48,128]{2,1,0:T(8,128)S(1)} %solve.8), channel_id=1, replica_groups=mesh['y'=4,'z'=4,'xl'=2,'xh'=2,'co'=2] {'z','xl'}, dimensions={0} | all-to-all | bytes 393216 | tf_op jit(solution)/shard_map/all_to_all | solution.py:464
  154.3 8.5 %all_to_all.63.own_ref = f32[8,48,128]{2,1,0:T(8,128)S(1)} all-to-all(f32[8,48,128]{2,1,0:T(8,128)S(1)} %nonlinear.9), channel_id=1, replica_groups=mesh['y'=4,'z'=4,'xl'=2,'xh'=2,'co'=2] {'z','xl'}, dimensions={0} | all-to-all | bytes 393216 | tf_op jit(solution)/shard_map/all_to_all | solution.py:455
  162.8 4.8 %collective-permute-start.10 = (f32[6,48,128]{2,1,0:T(8,128)S(1)}, f32[6,48,128]{2,1,0:T(8,128)S(1)}, u32[]{:S(2)}, u32[]{:S(2)}) collective-permute-start(f32[6,48,128]{2,1,0:T(8,128)S(1)} %slice.24), channel_id=1, source_target_pairs={{32,64},{64,32},{36,68},{68,36},{40,72},{72,40},{44,76},{76,44},{4... | collective-permute-start | bytes 442376 | tf_op jit(solution)/shard_map/ppermute | solution.py:460
  167.8 3.0 %collective-permute-done.10.odd_swap_ref = f32[6,48,128]{2,1,0:T(8,128)S(1)} collective-permute-done((f32[6,48,128]{2,1,0:T(8,128)S(1)}, f32[6,48,128]{2,1,0:T(8,128)S(1)}, u32[]{:S(2)}, u32[]{:S(2)}) %collective-permute-start.10) | collective-permute-done | bytes 147488 | tf_op jit(solution)/shard_map/ppermute | solution.py:460
  173.7 7.9 %all_to_all.64.chunks_ref = f32[4,6,16,128]{3,2,1,0:T(8,128)S(1)} all-to-all(f32[4,6,16,128]{3,2,1,0:T(8,128)S(1)} %solve.9), channel_id=1, replica_groups=mesh['y'=4,'z'=4,'xl'=2,'xh'=2,'co'=2] {'y'}, dimensions={0} | all-to-all | bytes 393216 | tf_op jit(solution)/shard_map/all_to_all | solution.py:465
  (46 shorter events, 27.1 us)
Async XLA Ops:
  0.0 0.9 copy-start.3
  1.7 11.3 %copy-start.4 = (s32[24,9]{0,1:T(8,128)S(1)}, s32[24,9]{0,1:T(8,128)}, u32[]{:S(2)}) copy-start(s32[24,9]{0,1:T(8,128)} %param.9) | copy-start | bytes 2596
  1.7 18.5 %all-to-all-start = ((f32[32,16,128]{2,1,0:T(8,128)}), f32[32,16,128]{2,1,0:T(8,128)S(1)}, u32[]{:S(2)}, u32[]{:S(2)}) async-start(f32[32,16,128]{2,1,0:T(8,128)} %get-tuple-element.10), calls=%async_computation | async-start | bytes 524288 | tf_op jit(solution)/shard_map/all_to_all | solution.py:446
  13.0 7.2 %copy-start.1 = (bf16[256,256]{1,0:T(8,128)(2,1)S(1)}, bf16[256,256]{1,0:T(8,128)(2,1)}, u32[]{:S(2)}) copy-start(bf16[256,256]{1,0:T(8,128)(2,1)} %constant.45.clone.forward_ref) | copy-start | bytes 393220
  13.0 7.2 %copy-start.2 = (bf16[128,384]{1,0:T(8,128)(2,1)S(1)}, bf16[128,384]{1,0:T(8,128)(2,1)}, u32[]{:S(2)}) copy-start(bf16[128,384]{1,0:T(8,128)(2,1)} %constant.44.clone.inverse_ref) | copy-start | bytes 294916
  21.1 30.4 %collective-permute-start.2 = (f32[4,5,128,128]{3,2,1,0:T(8,128)S(1)}, f32[4,5,128,128]{3,2,1,0:T(8,128)S(1)}, u32[]{:S(2)}, u32[]{:S(2)}) collective-permute-start(f32[4,5,128,128]{3,2,1,0:T(8,128)S(1)} %get-tuple-element.14), channel_id=1, source_target_pairs={{96,97},{97,96},{100,101},{101,100},{104,105},{105,104},{108,109},... | collective-permute-start | bytes 3932168 | tf_op jit(solution)/shard_map/ppermute | solution.py:452
  35.2 16.7 %collective-permute-start.1 = (f32[6,48,128]{2,1,0:T(8,128)}, f32[6,48,128]{2,1,0:T(8,128)S(1)}, u32[]{:S(2)}, u32[]{:S(2)}) collective-permute-start(f32[6,48,128]{2,1,0:T(8,128)} %slice.20), channel_id=1, source_target_pairs={{32,64},{64,32},{36,68},{68,36},{40,72},{72,40},{44,76},{76,44},{4... | collective-permute-start | bytes 442376 | tf_op jit(solution)/shard_map/ppermute | solution.py:460
  39.1 12.8 %collective-permute-start = (f32[6,48,128]{2,1,0:T(8,128)}, f32[6,48,128]{2,1,0:T(8,128)S(1)}, u32[]{:S(2)}, u32[]{:S(2)}) collective-permute-start(f32[6,48,128]{2,1,0:T(8,128)} %slice.20), channel_id=1, source_target_pairs={{0,32},{32,0},{4,36},{36,4},{8,40},{40,8},{12,44},{44,12},{16,48},... | collective-permute-start | bytes 442376 | tf_op jit(solution)/shard_map/ppermute | solution.py:459
  39.2 5.0 %copy-start = (f32[24,9,128,128]{3,2,1,0:T(8,128)S(1)}, f32[24,9,128,128]{3,2,1,0:T(8,128)}, u32[]{:S(2)}) copy-start(f32[24,9,128,128]{3,2,1,0:T(8,128)} %blocks_ref.3) | copy-start | bytes 42467332
  72.0 8.1 %collective-permute-start.4 = (f32[6,48,128]{2,1,0:T(8,128)S(1)}, f32[6,48,128]{2,1,0:T(8,128)S(1)}, u32[]{:S(2)}, u32[]{:S(2)}) collective-permute-start(f32[6,48,128]{2,1,0:T(8,128)S(1)} %slice.21), channel_id=1, source_target_pairs={{32,64},{64,32},{36,68},{68,36},{40,72},{72,40},{44,76},{76,44},{4... | collective-permute-start | bytes 442376 | tf_op jit(solution)/shard_map/ppermute | solution.py:460
  77.4 4.1 %collective-permute-start.3 = (f32[6,48,128]{2,1,0:T(8,128)S(1)}, f32[6,48,128]{2,1,0:T(8,128)S(1)}, u32[]{:S(2)}, u32[]{:S(2)}) collective-permute-start(f32[6,48,128]{2,1,0:T(8,128)S(1)} %slice.21), channel_id=1, source_target_pairs={{0,32},{32,0},{4,36},{36,4},{8,40},{40,8},{12,44},{44,12},{16,48},... | collective-permute-start | bytes 442376 | tf_op jit(solution)/shard_map/ppermute | solution.py:459
  101.4 8.5 %collective-permute-start.6 = (f32[6,48,128]{2,1,0:T(8,128)S(1)}, f32[6,48,128]{2,1,0:T(8,128)S(1)}, u32[]{:S(2)}, u32[]{:S(2)}) collective-permute-start(f32[6,48,128]{2,1,0:T(8,128)S(1)} %slice.22), channel_id=1, source_target_pairs={{32,64},{64,32},{36,68},{68,36},{40,72},{72,40},{44,76},{76,44},{4... | collective-permute-start | bytes 442376 | tf_op jit(solution)/shard_map/ppermute | solution.py:460
  107.1 4.1 %collective-permute-start.5 = (f32[6,48,128]{2,1,0:T(8,128)S(1)}, f32[6,48,128]{2,1,0:T(8,128)S(1)}, u32[]{:S(2)}, u32[]{:S(2)}) collective-permute-start(f32[6,48,128]{2,1,0:T(8,128)S(1)} %slice.22), channel_id=1, source_target_pairs={{0,32},{32,0},{4,36},{36,4},{8,40},{40,8},{12,44},{44,12},{16,48},... | collective-permute-start | bytes 442376 | tf_op jit(solution)/shard_map/ppermute | solution.py:459
  132.0 8.7 %collective-permute-start.8 = (f32[6,48,128]{2,1,0:T(8,128)S(1)}, f32[6,48,128]{2,1,0:T(8,128)S(1)}, u32[]{:S(2)}, u32[]{:S(2)}) collective-permute-start(f32[6,48,128]{2,1,0:T(8,128)S(1)} %slice.23), channel_id=1, source_target_pairs={{32,64},{64,32},{36,68},{68,36},{40,72},{72,40},{44,76},{76,44},{4... | collective-permute-start | bytes 442376 | tf_op jit(solution)/shard_map/ppermute | solution.py:460
  137.9 4.1 %collective-permute-start.7 = (f32[6,48,128]{2,1,0:T(8,128)S(1)}, f32[6,48,128]{2,1,0:T(8,128)S(1)}, u32[]{:S(2)}, u32[]{:S(2)}) collective-permute-start(f32[6,48,128]{2,1,0:T(8,128)S(1)} %slice.23), channel_id=1, source_target_pairs={{0,32},{32,0},{4,36},{36,4},{8,40},{40,8},{12,44},{44,12},{16,48},... | collective-permute-start | bytes 442376 | tf_op jit(solution)/shard_map/ppermute | solution.py:459
  162.8 8.0 %collective-permute-start.10 = (f32[6,48,128]{2,1,0:T(8,128)S(1)}, f32[6,48,128]{2,1,0:T(8,128)S(1)}, u32[]{:S(2)}, u32[]{:S(2)}) collective-permute-start(f32[6,48,128]{2,1,0:T(8,128)S(1)} %slice.24), channel_id=1, source_target_pairs={{32,64},{64,32},{36,68},{68,36},{40,72},{72,40},{44,76},{76,44},{4... | collective-permute-start | bytes 442376 | tf_op jit(solution)/shard_map/ppermute | solution.py:460
  167.7 4.1 %collective-permute-start.9 = (f32[6,48,128]{2,1,0:T(8,128)S(1)}, f32[6,48,128]{2,1,0:T(8,128)S(1)}, u32[]{:S(2)}, u32[]{:S(2)}) collective-permute-start(f32[6,48,128]{2,1,0:T(8,128)S(1)} %slice.24), channel_id=1, source_target_pairs={{0,32},{32,0},{4,36},{36,4},{8,40},{40,8},{12,44},{44,12},{16,48},... | collective-permute-start | bytes 442376 | tf_op jit(solution)/shard_map/ppermute | solution.py:459
